TPU v7x, 512 devices: a whole 4x4x16 slice. The times are simulated.
512 devices in a mesh: wide: 64 (over z, x), narrow: 8 (over y, core).
Axes of the slice: x: 4, y: 4, z: 16, core: 2. Of those that a mesh axis runs over, the one named last changes fastest.
Arguments:
- features: bfloat16 [32768, 128], P(('wide', 'narrow')), may hold values from -6 to 6
- send_rows: int32 [64, 8, 64, 32], P('wide', 'narrow'), may hold values from 0 to 63
- send_count: int32 [64, 8, 64], P('wide', 'narrow'), may hold values from 1 to 32, as said below
- neighbors: int32 [32768, 16], P(('wide', 'narrow')), may hold values from 0 to 2111, as said below
- w_self: bfloat16 [128, 128], replicated, may hold values from -0.5 to 0.5
- w_neigh: bfloat16 [128, 128], replicated, may hold values from -0.5 to 0.5
- bias_hidden: float32 [128], replicated, may hold values from -4 to 4
- w_out: bfloat16 [128, 256], replicated, may hold values from -0.5 to 0.5
- bias_out: float32 [256], replicated, may hold values from -4 to 4
- tiles: bfloat16 [64, 8, 64, 128, 128], P('wide', 'narrow'), may hold values from 0 to 0.0171875, as said below
- tile_rows: int32 [64, 8, 64], P('wide', 'narrow'), may hold values from 0 to 3
- tile_cols: int32 [64, 8, 64], P('wide', 'narrow'), may hold values from 0 to 31
- tile_count: int32 [64, 8], P('wide', 'narrow'), may hold values from 8 to 64, as said below
- dangling: int32 [32768], P(('wide', 'narrow')), may hold values from 0 to 1, as said below
Outputs:
- propagated: float32 [32768, 256], P(('wide', 'narrow'))
Inputs may be any that keep to these rules, and one draw needn't show every extreme that they name: Slots of a boundary row list from send_count on are unused; in every draw some list is full. `neighbors`: an entry below 64 names a row of the node's own device; an entry 64 + p * 32 + c names slot c of the list that device (p, b) keeps for the node's partition, b being the node's narrow index, and c is then below that list's count. Slots from tile_count on are unused; some device uses all 64 slots in every draw. `tile_rows`: tile coordinates of a device may repeat; repeated tiles add. `tiles`: entries are nonnegative. `dangling`: 1 marks a node without out-edges.
All inputs are finite; a program needn't handle non-finite values.
Results may differ from a plain program's by a relative error of at most 0.0003.
Values may be sent and summed in bfloat16 or wider, within the bound.
No kernel may reach another device: no remote copies, remote signals or barrier semaphores. Data moves between devices by JAX's collectives and lax.ppermute only.
A program may use at most 64 MiB of HBM per device.

v0:
```python
import math

import jax
import jax.numpy as jnp
from jax import lax
from jax.sharding import PartitionSpec as P

ITERS = 3


teleport = 0.1
highest = lax.Precision.HIGHEST


def spread_rows(panels, tile_mats, tile_rows, tile_cols, usable, row_tiles):
    count_all = tile_mats.shape[0]
    tile_size = tile_mats.shape[1]
    block_size = math.gcd(count_all, 16)
    rounds = count_all // block_size
    columns = tuple(
        (column_panel.reshape(-1, tile_size, column_panel.shape[1]) for column_panel in panels)
    )
    placing = (tile_rows[:, None] == jnp.arange(row_tiles)[None, :]).astype(jnp.float32)

    def advance(totals, piece):
        matrices, picked, weights, placed = piece
        scaled = matrices.astype(jnp.float32) * weights[:, None, None]
        updated = []
        for total_now, column_set in zip(totals, columns):
            product = jnp.einsum("tuv,tvc->tuc", scaled, column_set[picked], precision=highest)
            updated.append(
                total_now + jnp.einsum("tr,tuc->ruc", placed, product, precision=highest)
            )
        return (tuple(updated), None)

    initial = tuple(
        (
            jnp.zeros((row_tiles, tile_size, column_set.shape[2]), jnp.float32)
            for column_set in columns
        )
    )
    pieces = (
        tile_mats.reshape(rounds, block_size, tile_size, tile_size),
        tile_cols.reshape(rounds, block_size),
        usable.reshape(rounds, block_size),
        placing.reshape(rounds, block_size, row_tiles),
    )
    totals, _ = lax.scan(advance, initial, pieces)
    return tuple((total_now.reshape(row_tiles * tile_size, -1) for total_now in totals))


def body(
    features,
    send_rows,
    send_count,
    neighbors,
    w_self,
    w_neigh,
    bias_hidden,
    w_out,
    bias_out,
    tiles,
    tile_rows,
    tile_cols,
    tile_count,
    dangling,
):
    node_dev = features.shape[0]
    width_in = features.shape[1]
    partitions = lax.axis_size("wide")
    grid_cols = lax.axis_size("narrow")
    node_total = node_dev * partitions * grid_cols
    capacity = send_rows.shape[-1]
    tile_size = tiles.shape[-1]
    row_tiles = grid_cols * node_dev // tile_size
    outgoing = features[send_rows[0, 0]]
    slot_used = jnp.arange(capacity)[None, :] < send_count[0, 0][:, None]
    outgoing = jnp.where(slot_used[:, :, None], outgoing, jnp.zeros((), jnp.bfloat16))
    received = lax.all_to_all(outgoing, "wide", split_axis=0, concat_axis=0, tiled=True)
    self_term = jnp.dot(features, w_self, preferred_element_type=jnp.float32)
    row_pool = jnp.concatenate([features, received.reshape(-1, width_in)], axis=0)
    aggregate = (
        jnp.sum(row_pool[neighbors].astype(jnp.float32), axis=1) / neighbors.shape[1]
    ).astype(jnp.bfloat16)
    hidden = jax.nn.relu(
        self_term + jnp.dot(aggregate, w_neigh, preferred_element_type=jnp.float32) + bias_hidden
    )
    out_weight = w_out.astype(jnp.float32)
    weight_mask = dangling.astype(jnp.float32)
    tile_mats = tiles[0, 0]
    local_rows = tile_rows[0, 0]
    local_cols = tile_cols[0, 0]
    usable = (jnp.arange(tile_mats.shape[0]) < tile_count[0, 0]).astype(jnp.float32)
    logits = jnp.dot(hidden, out_weight, precision=highest) + bias_out
    carried = logits
    for repeat in range(ITERS):
        dangling_sum = lax.psum(
            jnp.dot(weight_mask, carried, precision=highest), ("wide", "narrow")
        )
        gathered = lax.all_gather(carried, "wide", axis=0, tiled=True)
        (partial_value,) = spread_rows(
            (gathered,), tile_mats, local_rows, local_cols, usable, row_tiles
        )
        summed = lax.psum_scatter(partial_value, "narrow", scatter_dimension=0, tiled=True)
        summed = summed + dangling_sum[None, :] / node_total
        carried = (1.0 - teleport) * summed + teleport * logits
    return carried


def solution(mesh):
    in_specs = (
        P(("wide", "narrow"), None),
        P("wide", "narrow", None, None),
        P("wide", "narrow", None),
        P(("wide", "narrow"), None),
        P(),
        P(),
        P(),
        P(),
        P(),
        P("wide", "narrow", None, None, None),
        P("wide", "narrow", None),
        P("wide", "narrow", None),
        P("wide", "narrow"),
        P(("wide", "narrow")),
    )
    out_specs = P(("wide", "narrow"), None)
    return jax.shard_map(body, mesh=mesh, in_specs=in_specs, out_specs=out_specs, check_vma=False)
```

profile of v0, /device:TPU:1, one launch (start us, length us, event | category | flops | bytes accessed | tf_op | source)
XLA Modules:
  0.0 932.2 jit_solution(15167640573413240289)
XLA Ops:
  6.5 0.8 compare_select_fusion.3
  7.5 0.7 iota_compare_fusion
  8.2 6.2 gather_fusion.3
  14.4 1.1 broadcast_select_fusion
  15.6 19.1 %all-to-all-start = ((bf16[64,32,128]{2,1,0:T(8,128)(2,1)}), bf16[64,32,128]{2,1,0:T(8,128)(2,1)S(1)}, u32[]{:S(2)}, u32[]{:S(2)}) async-start(bf16[64,32,128]{2,1,0:T(8,128)(2,1)} %broadcast_select_fusion), calls=%async_computation | async-start | bytes 1048576 | tf_op jit(solution)/shard_map/all_to_all | solution.py:79
  35.1 29.6 %all-to-all-done = bf16[64,32,128]{2,1,0:T(8,128)(2,1)S(1)} async-done(((bf16[64,32,128]{2,1,0:T(8,128)(2,1)}), bf16[64,32,128]{2,1,0:T(8,128)(2,1)S(1)}, u32[]{:S(2)}, u32[]{:S(2)}) %all-to-all-start) | async-done | bytes 524320 | tf_op jit(solution)/shard_map/all_to_all | solution.py:79
  64.8 3.2 gather_fusion.4
  68.2 0.8 convolution_add_fusion
  69.1 0.5 broadcast.188
  69.6 0.6 reduce.6
  70.3 0.6 reduce.7
  71.6 130.8 %all-gather.4.cloned.1.call-done = f32[4096,256]{1,0:T(8,128)} async-done(((f32[64,256]{1,0:T(8,128)}), f32[4096,256]{1,0:T(8,128)}) %all-gather.4.cloned.1.call-update) | async-done | bytes 4194320 | tf_op jit(solution)/shard_map/all_gather | solution.py:100
  202.5 42.2 %while.33 = (s32[]{:T(128)}, f32[4,128,256]{2,0,1:T(4,128)S(1)}, f32[4,16,4]{1,2,0:T(4,128)S(1)}, bf16[4,16,128,128]{3,2,1,0:T(8,128)(2,1)}, f32[4,16]{1,0:T(4,1...) while((s32[]{:T(128)}, f32[4,128,256]{2,0,1:T(4,128)S(1)}, ...), condition=%wide.region_2.3_spmd.clone, body=%wide.region_1.2_spmd.clone.sunk | while | flops 831259712 | bytes 12065843 | solution.py:48
  202.5 4.2 gather_fusion
  206.7 3.7 fusion.101
  210.5 2.6 fusion.102
  213.1 4.2 gather_fusion
  217.3 3.7 fusion.101
  221.0 2.6 fusion.102
  223.6 4.2 gather_fusion
  227.8 3.7 fusion.101
  231.6 2.6 fusion.102
  234.2 4.2 gather_fusion
  238.4 3.7 fusion.101
  242.1 2.6 fusion.102
  244.7 0.9 copy.20
  245.7 0.1 fusion.57
  245.8 108.5 %psum.21 = f32[256]{0:T(256)S(1)} all-reduce(f32[256]{0:T(256)S(1)} %bitcast.149), channel_id=1, replica_groups=mesh['wide'=64,'narrow'=8] {'wide','narrow'}, use_global_device_ids=true, to_apply=%region_4.5 | all-reduce | flops 256 | bytes 2048 | tf_op jit(solution)/shard_map/psum | solution.py:97
  354.4 1.5 multiply_add_fusion.2
  355.9 0.2 reduce-scatter.6.cloned.1.call-start
  356.1 131.2 %all-gather.6.cloned.1.call-done = f32[4096,256]{1,0:T(8,128)} async-done(((f32[64,256]{1,0:T(8,128)}), f32[4096,256]{1,0:T(8,128)}) %all-gather.6.cloned.1.call-update) | async-done | bytes 4194320 | tf_op jit(solution)/shard_map/all_gather | solution.py:100
  487.3 42.2 %while.34 = (s32[]{:T(128)}, f32[4,128,256]{2,0,1:T(4,128)S(1)}, f32[4,16,4]{1,2,0:T(4,128)S(1)}, bf16[4,16,128,128]{3,2,1,0:T(8,128)(2,1)}, f32[4,16]{1,0:T(4,1...) while((s32[]{:T(128)}, f32[4,128,256]{2,0,1:T(4,128)S(1)}, ...), condition=%wide.region_6.7_spmd.clone, body=%wide.region_5.6_spmd.clone.sunk | while | flops 831259712 | bytes 12065843 | solution.py:48
  487.3 4.2 gather_fusion.1
  491.5 3.7 fusion.108
  495.3 2.6 fusion.109
  497.9 4.2 gather_fusion.1
  502.1 3.7 fusion.108
  505.8 2.6 fusion.109
  508.4 4.2 gather_fusion.1
  512.6 3.7 fusion.108
  516.4 2.6 fusion.109
  519.0 4.2 gather_fusion.1
  523.2 3.7 fusion.108
  526.9 2.6 fusion.109
  529.5 0.9 copy.21
  530.6 108.5 %psum.22 = f32[256]{0:T(256)S(1)} all-reduce(f32[256]{0:T(256)S(1)} %bitcast.147), channel_id=1, replica_groups=mesh['wide'=64,'narrow'=8] {'wide','narrow'}, use_global_device_ids=true, to_apply=%region_8.9 | all-reduce | flops 256 | bytes 2048 | tf_op jit(solution)/shard_map/psum | solution.py:97
  639.2 1.5 multiply_add_fusion.1
  640.7 131.3 %all-gather.8.cloned.1.call-done = f32[4096,256]{1,0:T(8,128)} async-done(((f32[64,256]{1,0:T(8,128)}), f32[4096,256]{1,0:T(8,128)}) %all-gather.8.cloned.1.call-update) | async-done | bytes 4194320 | tf_op jit(solution)/shard_map/all_gather | solution.py:100
  772.1 42.2 %while.35 = (s32[]{:T(128)}, f32[4,128,256]{2,0,1:T(4,128)S(1)}, f32[4,16,4]{1,2,0:T(4,128)S(1)}, bf16[4,16,128,128]{3,2,1,0:T(8,128)(2,1)}, f32[4,16]{1,0:T(4,1...) while((s32[]{:T(128)}, f32[4,128,256]{2,0,1:T(4,128)S(1)}, ...), condition=%wide.region_10.11_spmd.clone, body=%wide.region_9.10_spmd.clone.sunk | while | flops 831259712 | bytes 12065843 | solution.py:48
  772.1 4.2 gather_fusion.2
  776.3 3.7 fusion.115
  780.0 2.6 fusion.116
  782.7 4.2 gather_fusion.2
  786.9 3.7 fusion.115
  790.6 2.6 fusion.116
  793.2 4.2 gather_fusion.2
  797.4 3.7 fusion.115
  801.1 2.6 fusion.116
  803.8 4.2 gather_fusion.2
  808.0 3.7 fusion.115
  811.7 2.6 fusion.116
  814.3 0.9 copy.22
  815.4 108.5 %psum.23 = f32[256]{0:T(256)S(1)} all-reduce(f32[256]{0:T(256)S(1)} %bitcast.148), channel_id=1, replica_groups=mesh['wide'=64,'narrow'=8] {'wide','narrow'}, use_global_device_ids=true, to_apply=%region_12.13 | all-reduce | flops 256 | bytes 2048 | tf_op jit(solution)/shard_map/psum | solution.py:97
  923.9 1.5 multiply_add_fusion
  (99 shorter events, 1.8 us)
Async XLA Ops:
  6.5 61.7 %copy-start = (bf16[128,256]{1,0:T(8,128)(2,1)S(1)}, bf16[128,256]{1,0:T(8,128)(2,1)}, u32[]{:S(2)}) copy-start(bf16[128,256]{1,0:T(8,128)(2,1)} %param.27) | copy-start | bytes 196612
  6.5 1.7 copy-start.1
  14.4 20.4 %copy-start.7 = (s32[64,16]{0,1:T(8,128)S(1)}, s32[64,16]{0,1:T(8,128)}, u32[]{:S(2)}) copy-start(s32[64,16]{0,1:T(8,128)} %param.23) | copy-start | bytes 12292
  14.4 20.6 %copy-start.5 = (bf16[128,128]{1,0:T(8,128)(2,1)S(1)}, bf16[128,128]{1,0:T(8,128)(2,1)}, u32[]{:S(2)}) copy-start(bf16[128,128]{1,0:T(8,128)(2,1)} %param.24) | copy-start | bytes 98308
  15.6 49.1 %all-to-all-start = ((bf16[64,32,128]{2,1,0:T(8,128)(2,1)}), bf16[64,32,128]{2,1,0:T(8,128)(2,1)S(1)}, u32[]{:S(2)}, u32[]{:S(2)}) async-start(bf16[64,32,128]{2,1,0:T(8,128)(2,1)} %broadcast_select_fusion), calls=%async_computation | async-start | bytes 1048576 | tf_op jit(solution)/shard_map/all_to_all | solution.py:79
  34.7 33.4 %copy-start.6 = (bf16[128,128]{1,0:T(8,128)(2,1)S(1)}, bf16[128,128]{1,0:T(8,128)(2,1)}, u32[]{:S(2)}) copy-start(bf16[128,128]{1,0:T(8,128)(2,1)} %param.25) | copy-start | bytes 98308
  34.7 33.4 %copy-start.10 = (f32[128]{0:T(128)S(1)}, f32[128]{0:T(128)}, u32[]{:S(2)}) copy-start(f32[128]{0:T(128)} %param.26) | copy-start | bytes 1540
  34.7 33.5 %copy-start.9 = (f32[256]{0:T(256)S(1)}, f32[256]{0:T(256)}, u32[]{:S(2)}) copy-start(f32[256]{0:T(256)} %param.28) | copy-start | bytes 3076
  34.7 167.7 %all-gather.4.cloned.1.call-start = ((), (), s32[]{:S(2)}) async-start(), calls=%async_computation.4 | async-start | bytes 4259840 | tf_op jit(solution)/shard_map/all_gather | solution.py:100
  35.0 34.7 %copy-start.11 = (s32[1,1,64]{2,1,0:T(1,128)S(1)}, s32[1,1,64]{2,1,0:T(1,128)}, u32[]{:S(2)}) copy-start(s32[1,1,64]{2,1,0:T(1,128)} %param.30) | copy-start | bytes 772
  35.0 35.3 %copy-start.12 = (s32[1,1,64]{2,1,0:T(1,128)S(1)}, s32[1,1,64]{2,1,0:T(1,128)}, u32[]{:S(2)}) copy-start(s32[1,1,64]{2,1,0:T(1,128)} %param.31) | copy-start | bytes 772
  69.1 285.3 %reduce-scatter.4.cloned.1.call-start = ((), (), s32[]{:S(2)}) async-start(), calls=%async_computation.5 | async-start | bytes 589824 | tf_op jit(solution)/shard_map/reduce_scatter | solution.py:104
  202.5 43.2 %copy-start.2 = (f32[64,256]{1,0:T(8,128)S(1)}, f32[64,256]{1,0:T(8,128)}, u32[]{:S(2)}) copy-start(f32[64,256]{1,0:T(8,128)} %convolution_add_fusion) | copy-start | bytes 196612
  202.5 43.2 %copy-start.8 = (s32[64]{0:T(128)S(1)}, s32[64]{0:T(128)}, u32[]{:S(2)}) copy-start(s32[64]{0:T(128)} %param.33) | copy-start | bytes 772
  245.6 241.6 %all-gather.6.cloned.1.call-start = ((), (), s32[]{:S(2)}) async-start(), calls=%async_computation.6 | async-start | bytes 4259840 | tf_op jit(solution)/shard_map/all_gather | solution.py:100
  355.9 283.3 %reduce-scatter.6.cloned.1.call-start = ((), (), s32[]{:S(2)}) async-start(), calls=%async_computation.7 | async-start | bytes 589824 | tf_op jit(solution)/shard_map/reduce_scatter | solution.py:104
  487.3 43.2 %copy-start.4 = (f32[64,256]{1,0:T(8,128)S(1)}, f32[64,256]{1,0:T(8,128)}, u32[]{:S(2)}) copy-start(f32[64,256]{1,0:T(8,128)} %multiply_add_fusion.2) | copy-start | bytes 196612
  530.4 241.6 %all-gather.8.cloned.1.call-start = ((), (), s32[]{:S(2)}) async-start(), calls=%async_computation.8 | async-start | bytes 4259840 | tf_op jit(solution)/shard_map/all_gather | solution.py:100
  640.7 283.2 %reduce-scatter.8.cloned.1.call-start = ((), (), s32[]{:S(2)}) async-start(), calls=%async_computation.9 | async-start | bytes 589824 | tf_op jit(solution)/shard_map/reduce_scatter | solution.py:104
  772.1 43.2 %copy-start.3 = (f32[64,256]{1,0:T(8,128)S(1)}, f32[64,256]{1,0:T(8,128)}, u32[]{:S(2)}) copy-start(f32[64,256]{1,0:T(8,128)} %multiply_add_fusion.1) | copy-start | bytes 196612
Sparse Core Ops, SparseCore 0:
  69.2 133.2 all-gather.3
  245.8 39.9 reduce-scatter.3
  356.0 131.2 all-gather.5
  530.5 39.8 reduce-scatter.5
  640.8 131.2 all-gather.7
  815.3 39.8 reduce-scatter.7
where the time goes:
time: 934 us; the launch traced here: 932 us
  waiting for transfers between devices  423 us (45%)
  blocking collectives  326 us (35%)
  matrix products  77.2 us (8%)
  local copies, waits for them, and re-layouts  63.5 us (7%)
  starting transfers between devices  19.5 us (2%)
  between operations  14.4 us (2%)
    all_gather x3, waiting for transfers between devices, body(): gathered = lax.all_gather(carried, 'wide', axis=0, tiled=True)  393 us
    psum x3, blocking collectives, body(): lax.psum(jnp.dot(weight_mask, carried, precision=highest), ('wide', 'narr...  326 us
    gather x12, local copies, waits for them, and re-layouts, advance(): column_set[picked]  50.3 us
    dot_general x12, matrix products, advance(): jnp.einsum('tuv,tvc->tuc', scaled, column_set[picked], precision=highest)  44.7 us
    dot_general x12, matrix products, advance(): jnp.einsum('tr,tuc->ruc', placed, product, precision=highest)  31.1 us
    all_to_all x1, waiting for transfers between devices, body(): lax.all_to_all(outgoing, 'wide', split_axis=0, concat_axis=0, tiled=True)  29.6 us
    all_to_all x1, starting transfers between devices, body(): lax.all_to_all(outgoing, 'wide', split_axis=0, concat_axis=0, tiled=True)  19.1 us
  transfers between devices with their start and end apart: 7, of which 4 were waited for; matrix products, arithmetic and copies ran while one was open for 0% of the time, Pallas kernels for 0%

commit v1 on v0

v1 whole, which is shorter than its diff:
```python
import functools

import jax
import jax.numpy as jnp
from jax import lax
from jax.experimental import pallas as pl
from jax.experimental.pallas import tpu as pltpu
from jax.sharding import Mesh
from jax.sharding import PartitionSpec as P

ITERS = 3
TELEPORT = 0.1
TOP = 32767.0
TINY = 1e-30
INTERPRET = False

f32 = jnp.float32
bf16 = jnp.bfloat16
i32 = jnp.int32
i16 = jnp.int16


def call(body, out_shape, n_in, scratch=(), in_specs=None, flops=0, nbytes=0, limit=24 << 20):
    vmem = pl.BlockSpec(memory_space=pltpu.VMEM)
    outs = out_shape if isinstance(out_shape, (list, tuple)) else [out_shape]
    return pl.pallas_call(
        body,
        out_shape=out_shape,
        in_specs=in_specs or [vmem] * n_in,
        out_specs=[vmem] * len(outs) if isinstance(out_shape, (list, tuple)) else vmem,
        scratch_shapes=list(scratch),
        compiler_params=pltpu.CompilerParams(vmem_limit_bytes=limit),
        cost_estimate=pl.CostEstimate(flops=flops, bytes_accessed=nbytes, transcendentals=0),
        interpret=INTERPRET,
    )


def dot(a, b, dims=((1,), (0,))):
    return lax.dot_general(a, b, (dims, ((), ())), preferred_element_type=f32)


def split(x):
    hi = x.astype(bf16)
    return hi, (x - hi.astype(f32)).astype(bf16)


def encode(z, s, dangling, out_ref):
    nodes = z.shape[0]
    top = jnp.max(jnp.abs(z), axis=0, keepdims=True)
    dsum = jnp.sum(z * dangling[:nodes], axis=0, keepdims=True)
    ssum = jnp.sum(s * dangling[nodes : nodes + 1], axis=1, keepdims=True)
    row = lax.broadcasted_iota(i32, (8, z.shape[1]), 0)
    extra = jnp.where(row == 0, top, 0.0)
    extra = jnp.where(row == 1, s, extra)
    extra = jnp.where(row == 2, dsum, extra)
    extra = jnp.where(row == 3, ssum, extra)
    level = jnp.ceil(jnp.log2(jnp.maximum(jnp.abs(extra), TINY)) * 256.0)
    level = jnp.minimum(level, TOP)
    gain = TOP * jnp.exp2(level * (-1.0 / 256.0))
    codes = jnp.clip(jnp.round(z * gain[0:1]), -TOP, TOP).astype(i32)
    extra_codes = jnp.clip(jnp.round(extra * gain), -TOP, TOP).astype(i32)
    packed = jnp.concatenate([codes, level.astype(i32), extra_codes], axis=0).astype(i16)
    for k in range(out_ref.shape[0]):
        out_ref[k] = packed


def pick_kernel(index_ref, features_ref, out_ref):
    features = features_ref[...]
    nodes = features.shape[0]
    for k in range(index_ref.shape[0]):
        row = lax.broadcasted_iota(i32, (nodes, 128), 0)
        chosen = (row == index_ref[k : k + 1, :]).astype(f32).astype(bf16)
        out_ref[pl.ds(k * 128, 128), :] = dot(chosen, features, ((0,), (0,))).astype(bf16)


def panel_kernel(
    rows_ref, cols_ref, count_ref, tiles_ref, neighbors_ref, panel_ref, own_ref, far_ref, total
):
    row_tiles = panel_ref.shape[0] // 256
    col_tiles = panel_ref.shape[1] // 128
    zero = jnp.zeros((128, 128), f32)

    def clear(p, _):
        total[p] = zero
        return 0

    lax.fori_loop(0, row_tiles * col_tiles, clear, 0)

    def place(t, _):
        p = rows_ref[t] * col_tiles + cols_ref[t]
        total[p] = total[p] + tiles_ref[t].astype(f32)
        return 0

    lax.fori_loop(0, count_ref[0], place, 0)

    def store(r, _):
        for c in range(col_tiles):
            hi, lo = split(total[r * col_tiles + c])
            panel_ref[pl.ds(pl.multiple_of(r * 128, 128), 128), pl.ds(c * 128, 128)] = hi
            panel_ref[
                pl.ds(pl.multiple_of((r + row_tiles) * 128, 128), 128), pl.ds(c * 128, 128)
            ] = lo
        return 0

    lax.fori_loop(0, row_tiles, store, 0)

    nodes = own_ref.shape[0]
    degree = neighbors_ref.shape[1]
    linked = neighbors_ref[...]

    def counts(width, offset):
        slot = lax.broadcasted_iota(i32, (nodes, width), 1) + offset
        got = jnp.zeros((nodes, width), f32)
        for k in range(degree):
            got = got + jnp.where(linked[:, k : k + 1] == slot, 1.0, 0.0)
        return got.astype(bf16)

    own_ref[...] = counts(nodes, 0)
    for c in range(0, far_ref.shape[1], 256):
        far_ref[:, pl.ds(c, 256)] = counts(256, nodes + c)


def hidden_kernel(
    degree,
    features_ref,
    received_ref,
    own_ref,
    far_ref,
    w_self_ref,
    w_neigh_ref,
    bias_ref,
    dangling_ref,
    hidden_ref,
    out_ref,
):
    features = features_ref[...]
    pooled = dot(own_ref[...], features) + dot(far_ref[...], received_ref[...])
    aggregate = (pooled * (1.0 / degree)).astype(bf16)
    hidden = dot(features, w_self_ref[...]) + dot(aggregate, w_neigh_ref[...]) + bias_ref[...]
    hidden = jnp.maximum(hidden, 0.0)
    hidden_ref[...] = hidden
    encode(hidden, jnp.ones((1, hidden.shape[1]), f32), dangling_ref[...], out_ref)


def spread_kernel(
    node_total, parts, panel_hbm, packed_ref, out_ref, panel, z_parts, s_parts, sems
):
    zh, zl, nx = parts
    half = panel.shape[0] // 2
    loads = [
        pltpu.make_async_copy(
            panel_hbm.at[pl.ds(k * half, half)], panel.at[pl.ds(k * half, half)], sems.at[k]
        )
        for k in range(2)
    ]
    for load in loads:
        load.start()
    nodes = 64
    d_all = jnp.zeros((1, 128), f32)
    ds_all = jnp.zeros((1, 128), f32)
    lane = lax.broadcasted_iota(i32, (1, 128), 1)
    before = None
    for a in range(zh * zl * nx):
        h, m, x = a // (zl * nx), (a // nx) % zl, a % nx
        codes = packed_ref[x, m, h].astype(i32).astype(f32)
        step = jnp.exp2(codes[nodes : nodes + 8] * (1.0 / 256.0)) * (1.0 / TOP)
        hi, lo = split(codes[:nodes] * step[0:1])
        z_parts[pl.ds(a * nodes, nodes), pl.ds(0, 128)] = hi
        z_parts[pl.ds(a * nodes, nodes), pl.ds(128, 128)] = lo
        extra = codes[nodes + 8 : nodes + 16] * step
        d_all = d_all + extra[2:3]
        ds_all = ds_all + extra[3:4]
        if a % 2:
            hi, lo = split(jnp.where(lane < nodes, before, extra[1:2]))
            s_parts[:, pl.ds((a // 2) * 128, 128)] = jnp.concatenate(
                [hi.astype(f32), lo.astype(f32), jnp.zeros((14, 128), f32)], axis=0
            ).astype(bf16)
        before = extra[1:2]
    d_all = d_all * (1.0 / node_total)
    ds_all = ds_all * (1.0 / node_total)
    loads[0].wait()
    first = dot(panel[:half], z_parts[...])
    loads[1].wait()
    second = dot(panel[half:], z_parts[...])
    z_sum = (first[:, :128] + first[:, 128:]) + (second[:, :128] + second[:, 128:]) + d_all
    s_sum = dot(s_parts[...], panel[...], ((1,), (1,)))
    s_sum = (s_sum[0:1] + s_sum[1:2])
    s_sum = s_sum[:, :half] + s_sum[:, half:]
    for b in range(half // nodes):
        out_ref[b, pl.ds(0, nodes), :] = z_sum[b * nodes : (b + 1) * nodes]
        two = s_sum[:, (b // 2) * 128 : (b // 2) * 128 + 128]
        if b % 2:
            two = pltpu.roll(two, nodes, 1)
        out_ref[b, pl.ds(nodes, 8), :] = jnp.broadcast_to(two + ds_all, (8, 128))


def gather_step(received_ref, hidden_ref):
    nodes = hidden_ref.shape[0]
    total = received_ref[0]
    for j in range(1, received_ref.shape[0]):
        total = total + received_ref[j]
    z = (1.0 - TELEPORT) * total[:nodes] + TELEPORT * hidden_ref[...]
    s = (1.0 - TELEPORT) * total[nodes : nodes + 1] + TELEPORT
    return z, s


def step_kernel(received_ref, hidden_ref, dangling_ref, out_ref):
    z, s = gather_step(received_ref, hidden_ref)
    s8 = jnp.broadcast_to(s, (8, 128))
    lane = lax.broadcasted_iota(i32, (8, 128), 1)
    s8 = jnp.where(lane < z.shape[0], s8, pltpu.roll(s8, z.shape[0], 1))
    encode(z, s8[0:1], dangling_ref[...], out_ref)


def last_kernel(received_ref, hidden_ref, w_ref, bias_ref, out_ref):
    z, s = gather_step(received_ref, hidden_ref)
    nodes = z.shape[0]
    hi = z.astype(bf16)
    mid, lo = split(z - hi.astype(f32))
    w = w_ref[...]
    same = lax.broadcasted_iota(i32, (nodes, 128), 0) == lax.broadcasted_iota(i32, (nodes, 128), 1)
    column = jnp.sum(jnp.where(same, jnp.broadcast_to(s, (nodes, 128)), 0.0), axis=1, keepdims=True)
    out_ref[...] = (dot(lo, w) + dot(mid, w)) + dot(hi, w) + column * bias_ref[...]


def body(
    features,
    send_rows,
    send_count,
    neighbors,
    w_self,
    w_neigh,
    bias_hidden,
    w_out,
    bias_out,
    tiles,
    tile_rows,
    tile_cols,
    tile_count,
    dangling,
):
    shape = jax.ShapeDtypeStruct
    nodes, width = features.shape
    zh, zl, nx = (lax.axis_size(name) for name in ("zh", "zl", "x"))
    wide = zh * zl * nx
    narrow = lax.axis_size("narrow")
    capacity = send_rows.shape[-1]
    slots = wide * capacity
    row_total = narrow * nodes
    col_total = wide * nodes
    node_total = row_total * wide
    degree = neighbors.shape[1]

    used = jnp.arange(capacity)[None, :] < send_count[0, 0][:, None]
    index = jnp.where(used, send_rows[0, 0], -1).reshape(slots // 128, 128)
    outgoing = call(pick_kernel, shape((slots, width), bf16), 2)(index, features)
    received = lax.all_to_all(
        outgoing.reshape(wide, capacity, width),
        ("zh", "zl", "x"),
        split_axis=0,
        concat_axis=0,
        tiled=True,
    ).reshape(slots, width)

    smem = pl.BlockSpec(memory_space=pltpu.SMEM)
    vmem = pl.BlockSpec(memory_space=pltpu.VMEM)
    panel, own, far = call(
        panel_kernel,
        [
            shape((2 * row_total, col_total), bf16),
            shape((nodes, nodes), bf16),
            shape((nodes, slots), bf16),
        ],
        5,
        in_specs=[smem, smem, smem, vmem, vmem],
        scratch=[pltpu.VMEM((row_total * col_total // (128 * 128), 128, 128), f32)],
        flops=1 << 24,
        nbytes=20 << 20,
        limit=28 << 20,
    )(tile_rows[0, 0], tile_cols[0, 0], tile_count[0], tiles[0, 0], neighbors)

    mark = dangling.astype(f32)
    marks = jnp.concatenate(
        [
            jnp.broadcast_to(mark[:, None], (nodes, 128)),
            jnp.broadcast_to(jnp.pad(mark, (0, 128 - nodes))[None, :], (8, 128)),
        ],
        axis=0,
    )

    packed_shape = shape((zh, nodes + 16, width), i16)
    hidden, packed = call(
        functools.partial(hidden_kernel, degree),
        [shape((nodes, width), f32), packed_shape],
        8,
    )(features, received, own, far, w_self, w_neigh, bias_hidden[None, :], marks)

    spread = call(
        functools.partial(spread_kernel, node_total, (zh, zl, nx)),
        shape((narrow, nodes + 8, width), f32),
        2,
        in_specs=[pl.BlockSpec(memory_space=pl.ANY), vmem],
        scratch=[
            pltpu.VMEM((2 * row_total, col_total), bf16),
            pltpu.VMEM((col_total, 2 * width), bf16),
            pltpu.VMEM((16, col_total), bf16),
            pltpu.SemaphoreType.DMA((2,)),
        ],
        flops=2 * 2 * row_total * col_total * 256,
        nbytes=10 << 20,
    )
    for repeat in range(ITERS):
        got = lax.all_to_all(packed, "zh", split_axis=0, concat_axis=0, tiled=True)
        got = lax.all_to_all(
            jnp.broadcast_to(got[None], (zl,) + got.shape),
            "zl",
            split_axis=0,
            concat_axis=0,
            tiled=True,
        )
        got = lax.all_gather(got, "x", axis=0)
        partial = spread(panel, got)
        sums = lax.all_to_all(partial, "narrow", split_axis=0, concat_axis=0, tiled=True)
        if repeat < ITERS - 1:
            packed = call(step_kernel, packed_shape, 3)(sums, hidden, marks)
    return call(last_kernel, shape((nodes, w_out.shape[1]), f32), 4)(
        sums, hidden, w_out, bias_out[None, :]
    )


def solution(mesh):
    wide, narrow = mesh.devices.shape
    nx = 4 if wide % 64 == 0 else 2
    zl = 4 if wide % 64 == 0 else 2
    split_mesh = Mesh(
        mesh.devices.reshape(wide // (zl * nx), zl, nx, narrow), ("zh", "zl", "x", "narrow")
    )
    wide_axes = ("zh", "zl", "x")
    all_axes = wide_axes + ("narrow",)
    in_specs = (
        P(all_axes, None),
        P(wide_axes, "narrow", None, None),
        P(wide_axes, "narrow", None),
        P(all_axes, None),
        P(),
        P(),
        P(),
        P(),
        P(),
        P(wide_axes, "narrow", None, None, None),
        P(wide_axes, "narrow", None),
        P(wide_axes, "narrow", None),
        P(wide_axes, "narrow"),
        P(all_axes),
    )
    return jax.shard_map(
        body, mesh=split_mesh, in_specs=in_specs, out_specs=P(all_axes, None), check_vma=False
    )
```

time: 934 us -> 252 us (0.27)
  waiting for transfers between devices: 423 us -> 19.7 us
  blocking collectives: 326 us -> 168 us
  matrix products: 77.2 us -> 0 us
  local copies, waits for them, and re-layouts: 63.5 us -> 10.9 us
  Pallas kernels: 0 us -> 31.3 us
  between operations: 14.4 us -> 0.88 us
    all_gather x3 -> x0, waiting for transfers between devices: 393 us -> none  [body(): gathered = lax.all_gather(carried, 'wide', axis=0, tiled=True)]
    psum x3 -> x0, blocking collectives: 326 us -> none  [body(): lax.psum(jnp.dot(weight_mask, carried, precision=highest), ('wide', 'narr...]
    all_to_all x0 -> x9, blocking collectives: none -> 129 us  [the longest x3 53.8 us: body(): lax.all_to_all(partial, 'narrow', split_axis=0, concat_axis=0, tiled=True)]
    dot_general x30 -> x0, matrix products: 77.2 us -> none  [the longest x12 44.7 us: advance(): jnp.einsum('tuv,tvc->tuc', scaled, column_set[picked], precision=highest)]
    gather x14 -> x0, local copies, waits for them, and re-layouts: 59.7 us -> none  [the longest x12 50.3 us: advance(): column_set[picked]]
    all_gather x0 -> x3, blocking collectives: none -> 38.4 us  [body(): got = lax.all_gather(got, 'x', axis=0)]
    pallas_call x0 -> x9, Pallas kernels: none -> 31.3 us  [the longest x3 24 us: body(): partial = spread(panel, got)]
    all_to_all x1, waiting for transfers between devices: 29.6 us -> 19.7 us  [body(): lax.all_to_all(outgoing.reshape(wide, capacity, width), ('zh', 'zl', 'x')...]
  transfers between devices with their start and end apart: 7 -> 1, of which waited for: 4 -> 1; matrix products, arithmetic and copies ran while one was open for 0% -> 0% of each run, Pallas kernels for 0% -> 2%
where the time goes in v1:
time: 252 us; the launch traced here: 251 us
  blocking collectives  168 us (67%)
  Pallas kernels  31.3 us (12%)
  waiting for transfers between devices  19.7 us (8%)
  starting transfers between devices  19.2 us (8%)
  local copies, waits for them, and re-layouts  10.9 us (4%)
    all_to_all x3, blocking collectives, body(): lax.all_to_all(partial, 'narrow', split_axis=0, concat_axis=0, tiled=True)  53.8 us
    all_to_all x3, blocking collectives, body(): got = lax.all_to_all(packed, 'zh', split_axis=0, concat_axis=0, tiled=True)  47 us
    all_gather x3, blocking collectives, body(): got = lax.all_gather(got, 'x', axis=0)  38.4 us
    all_to_all x3, blocking collectives, body(): lax.all_to_all(jnp.broadcast_to(got[None], (zl,) + got.shape), 'zl', spli...  28.3 us
    pallas_call x3, Pallas kernels, body(): partial = spread(panel, got)  24 us
    all_to_all x1, waiting for transfers between devices, body(): lax.all_to_all(outgoing.reshape(wide, capacity, width), ('zh', 'zl', 'x')...  19.7 us
    all_to_all x1, starting transfers between devices, body(): lax.all_to_all(outgoing.reshape(wide, capacity, width), ('zh', 'zl', 'x')...  19.2 us
    unnamed x33, local copies, waits for them, and re-layouts  10.4 us
  transfers between devices with their start and end apart: 1, of which 1 were waited for; matrix products, arithmetic and copies ran while one was open for 0% of the time, Pallas kernels for 2%

profile of v1, /device:TPU:1, one launch (start us, length us, event | category | flops | bytes accessed | tf_op | source)
XLA Modules:
  0.0 251.0 jit_solution(7703600596560636659)
XLA Ops:
  0.0 0.0 copy-start.14
  0.0 0.0 copy-start.13
  0.0 0.0 copy-start.11
  0.0 0.0 copy-start.10
  0.0 0.1 lt.23
  0.1 0.5 broadcast.16
  0.6 1.3 reduce.3
  1.9 0.1 lt.25
  2.0 0.1 lt.26
  2.1 0.1 lt.27
  2.2 0.8 copy.20
  3.0 0.1 squeeze.19
  3.1 0.0 copy-start.4
  3.1 0.7 copy-done.4
  3.8 1.2 shard_map.137
  5.0 0.0 copy-start.8
  5.0 19.2 %all-to-all-start = ((bf16[64,32,128]{2,1,0:T(8,128)(2,1)}), bf16[64,32,128]{2,1,0:T(8,128)(2,1)S(1)}, u32[]{:S(2)}, u32[]{:S(2)}) async-start(bf16[64,32,128]{2,1,0:T(8,128)(2,1)} %bitcast.4), calls=%async_computation | async-start | bytes 1048576 | tf_op jit(solution)/shard_map/all_to_all | solution.py:257
  24.2 0.0 copy-start.5
  24.2 0.0 copy-start.7
  24.3 0.0 copy-start.12
  24.9 0.0 copy-done.14
  25.0 0.0 copy-done.13
  25.0 0.1 copy.19.neighbors_ref
  25.1 0.0 copy-done.11
  25.1 0.0 copy-done.10
  25.1 0.0 copy-start.3
  25.1 1.6 copy-done.3
  26.7 4.5 %shard_map.136 = (bf16[1024,4096]{1,0:T(8,128)(2,1)S(1)}, bf16[64,64]{1,0:T(8,128)(2,1)S(1)}, bf16[64,2048]{1,0:T(8,128)(2,1)S(1)}) custom-call(s32[64]{0:T(128)S(1)} %bitcast.20, s32[64]{0:T(128)S(1)} %bitcast.21, s32[1]{0:T(128)} %bitcast.13.count_ref, bf16[64,128,128]{2,1,0:T(8,128)(2,1)S(1)} %bitcast.17, s32[64,16]{1,0:T(8,128)S(1)} %copy.19.neighbors_ref), custom_call_target="tpu_custom_call" | custom-call | flops 16777216 | bytes 20971520 | tf_op jit(solution)/shard_map/pallas_call | solution.py:267
  31.2 0.0 copy-start
  31.2 3.2 %copy-done = bf16[1024,4096]{1,0:T(8,128)(2,1)} copy-done((bf16[1024,4096]{1,0:T(8,128)(2,1)}, bf16[1024,4096]{1,0:T(8,128)(2,1)S(1)}, u32[]{:S(2)}) %copy-start) | copy-done | bytes 8388632
  34.4 0.1 pad_maximum_fusion.dangling_ref
  34.5 19.7 %all-to-all-done = bf16[64,32,128]{2,1,0:T(8,128)(2,1)S(1)} async-done(((bf16[64,32,128]{2,1,0:T(8,128)(2,1)}), bf16[64,32,128]{2,1,0:T(8,128)(2,1)S(1)}, u32[]{:S(2)}, u32[]{:S(2)}) %all-to-all-start) | async-done | bytes 524320 | tf_op jit(solution)/shard_map/all_to_all | solution.py:257
  54.3 0.0 copy-done.8
  54.3 0.0 copy-done.5
  54.3 0.0 copy-done.7
  54.3 0.0 copy-done.12
  54.3 0.4 shard_map.138
  54.7 17.1 %all_to_all.50 = s16[4,80,128]{2,1,0:T(8,128)(2,1)S(1)} all-to-all(s16[4,80,128]{2,1,0:T(8,128)(2,1)S(1)} %get-tuple-element.13), channel_id=1, replica_groups=mesh['zh'=4,'zl'=4,'x'=4,'narrow'=8] {'zh'}, dimensions={0} | all-to-all | bytes 163840 | tf_op jit(solution)/shard_map/all_to_all | solution.py:313
  71.8 9.5 %all_to_all.51 = s16[4,4,80,128]{3,2,1,0:T(8,128)(2,1)S(1)} all-to-all(s16[4,4,80,128]{3,2,1,0:T(8,128)(2,1)S(1)} %broadcast_in_dim.22), channel_id=1, replica_groups=mesh['zh'=4,'zl'=4,'x'=4,'narrow'=8] {'zl'}, dimensions={0} | all-to-all | bytes 655360 | tf_op jit(solution)/shard_map/all_to_all | solution.py:314
  81.3 13.3 %all-gather.6 = s16[16,4,80,128]{3,2,1,0:T(8,128)(2,1)S(1)} all-gather(s16[4,4,80,128]{3,2,1,0:T(8,128)(2,1)S(1)} %all_to_all.51), channel_id=2, replica_groups=mesh['zh'=4,'zl'=4,'x'=4,'narrow'=8] {'x'}, dimensions={0}, use_global_device_ids=true | all-gather | bytes 1638400 | tf_op jit(solution)/shard_map/all_gather | solution.py:321
  94.6 0.0 copy-start.1
  94.6 3.4 %copy-done.1 = bf16[1024,4096]{1,0:T(8,128)(2,1)S(1)} copy-done((bf16[1024,4096]{1,0:T(8,128)(2,1)S(1)}, bf16[1024,4096]{1,0:T(8,128)(2,1)}, u32[]{:S(2)}) %copy-start.1) | copy-done | bytes 8388632
  98.0 0.0 copy-start.2
  98.0 8.0 %shard_map.139 = f32[8,72,128]{2,1,0:T(8,128)S(1)} custom-call(bf16[1024,4096]{1,0:T(8,128)(2,1)S(1)} %copy-done.1, s16[4,4,4,80,128]{4,3,2,1,0:T(8,128)(2,1)S(1)} %bitcast.14), custom_call_target="tpu_custom_call" | custom-call | flops 2147483648 | bytes 10485760 | tf_op jit(solution)/shard_map/pallas_call | solution.py:322
  106.0 19.5 %all_to_all.52.received_ref = f32[8,72,128]{2,1,0:T(8,128)S(1)} all-to-all(f32[8,72,128]{2,1,0:T(8,128)S(1)} %shard_map.139), channel_id=1, replica_groups=mesh['zh'=4,'zl'=4,'x'=4,'narrow'=8] {'narrow'}, dimensions={0} | all-to-all | bytes 589824 | tf_op jit(solution)/shard_map/all_to_all | solution.py:323
  125.5 0.2 shard_map.140
  125.7 14.5 %all_to_all.53 = s16[4,80,128]{2,1,0:T(8,128)(2,1)S(1)} all-to-all(s16[4,80,128]{2,1,0:T(8,128)(2,1)S(1)} %shard_map.140), channel_id=1, replica_groups=mesh['zh'=4,'zl'=4,'x'=4,'narrow'=8] {'zh'}, dimensions={0} | all-to-all | bytes 163840 | tf_op jit(solution)/shard_map/all_to_all | solution.py:313
  140.3 9.3 %all_to_all.54 = s16[4,4,80,128]{3,2,1,0:T(8,128)(2,1)S(1)} all-to-all(s16[4,4,80,128]{3,2,1,0:T(8,128)(2,1)S(1)} %broadcast_in_dim.23), channel_id=1, replica_groups=mesh['zh'=4,'zl'=4,'x'=4,'narrow'=8] {'zl'}, dimensions={0} | all-to-all | bytes 655360 | tf_op jit(solution)/shard_map/all_to_all | solution.py:314
  149.5 12.8 %all-gather.7 = s16[16,4,80,128]{3,2,1,0:T(8,128)(2,1)S(1)} all-gather(s16[4,4,80,128]{3,2,1,0:T(8,128)(2,1)S(1)} %all_to_all.54), channel_id=3, replica_groups=mesh['zh'=4,'zl'=4,'x'=4,'narrow'=8] {'x'}, dimensions={0}, use_global_device_ids=true | all-gather | bytes 1638400 | tf_op jit(solution)/shard_map/all_gather | solution.py:321
  162.3 0.0 copy-done.2
  162.3 8.0 %shard_map.141 = f32[8,72,128]{2,1,0:T(8,128)S(1)} custom-call(bf16[1024,4096]{1,0:T(8,128)(2,1)S(1)} %copy-done.2, s16[4,4,4,80,128]{4,3,2,1,0:T(8,128)(2,1)S(1)} %bitcast.16), custom_call_target="tpu_custom_call" | custom-call | flops 2147483648 | bytes 10485760 | tf_op jit(solution)/shard_map/pallas_call | solution.py:322
  170.3 17.0 %all_to_all.55.received_ref = f32[8,72,128]{2,1,0:T(8,128)S(1)} all-to-all(f32[8,72,128]{2,1,0:T(8,128)S(1)} %shard_map.141), channel_id=1, replica_groups=mesh['zh'=4,'zl'=4,'x'=4,'narrow'=8] {'narrow'}, dimensions={0} | all-to-all | bytes 589824 | tf_op jit(solution)/shard_map/all_to_all | solution.py:323
  187.3 0.2 shard_map.142
  187.5 15.4 %all_to_all.56 = s16[4,80,128]{2,1,0:T(8,128)(2,1)S(1)} all-to-all(s16[4,80,128]{2,1,0:T(8,128)(2,1)S(1)} %shard_map.142), channel_id=1, replica_groups=mesh['zh'=4,'zl'=4,'x'=4,'narrow'=8] {'zh'}, dimensions={0} | all-to-all | bytes 163840 | tf_op jit(solution)/shard_map/all_to_all | solution.py:313
  202.9 9.6 %all_to_all.57 = s16[4,4,80,128]{3,2,1,0:T(8,128)(2,1)S(1)} all-to-all(s16[4,4,80,128]{3,2,1,0:T(8,128)(2,1)S(1)} %broadcast_in_dim.24), channel_id=1, replica_groups=mesh['zh'=4,'zl'=4,'x'=4,'narrow'=8] {'zl'}, dimensions={0} | all-to-all | bytes 655360 | tf_op jit(solution)/shard_map/all_to_all | solution.py:314
  212.5 12.4 %all-gather.8 = s16[16,4,80,128]{3,2,1,0:T(8,128)(2,1)S(1)} all-gather(s16[4,4,80,128]{3,2,1,0:T(8,128)(2,1)S(1)} %all_to_all.57), channel_id=4, replica_groups=mesh['zh'=4,'zl'=4,'x'=4,'narrow'=8] {'x'}, dimensions={0}, use_global_device_ids=true | all-gather | bytes 1638400 | tf_op jit(solution)/shard_map/all_gather | solution.py:321
  224.9 0.0 copy-start.6
  224.9 0.0 copy-start.9
  224.9 8.0 %shard_map.143 = f32[8,72,128]{2,1,0:T(8,128)S(1)} custom-call(bf16[1024,4096]{1,0:T(8,128)(2,1)S(1)} %copy-done.2, s16[4,4,4,80,128]{4,3,2,1,0:T(8,128)(2,1)S(1)} %bitcast.15), custom_call_target="tpu_custom_call" | custom-call | flops 2147483648 | bytes 10485760 | tf_op jit(solution)/shard_map/pallas_call | solution.py:322
  232.9 17.3 %all_to_all.58.received_ref = f32[8,72,128]{2,1,0:T(8,128)S(1)} all-to-all(f32[8,72,128]{2,1,0:T(8,128)S(1)} %shard_map.143), channel_id=1, replica_groups=mesh['zh'=4,'zl'=4,'x'=4,'narrow'=8] {'narrow'}, dimensions={0} | all-to-all | bytes 589824 | tf_op jit(solution)/shard_map/all_to_all | solution.py:323
  250.2 0.0 copy-done.6
  250.2 0.0 copy-done.9
  250.2 0.8 shard_map.144
  (9 shorter events, 0.2 us)
Async XLA Ops:
  0.0 24.9 %copy-start.14 = (s32[64]{0:T(128)S(1)}, s32[64]{0:T(128)}, u32[]{:S(2)}) copy-start(s32[64]{0:T(128)} %param.27) | copy-start | bytes 772
  0.0 25.0 %copy-start.13 = (s32[64,16]{0,1:T(8,128)S(1)}, s32[64,16]{0,1:T(8,128)}, u32[]{:S(2)}) copy-start(s32[64,16]{0,1:T(8,128)} %param.17) | copy-start | bytes 12292
  0.0 25.1 %copy-start.11 = (s32[1,1,64]{2,1,0:T(1,128)S(1)}, s32[1,1,64]{2,1,0:T(1,128)}, u32[]{:S(2)}) copy-start(s32[1,1,64]{2,1,0:T(1,128)} %param.25) | copy-start | bytes 772
  0.0 25.1 %copy-start.10 = (s32[1,1,64]{2,1,0:T(1,128)S(1)}, s32[1,1,64]{2,1,0:T(1,128)}, u32[]{:S(2)}) copy-start(s32[1,1,64]{2,1,0:T(1,128)} %param.24) | copy-start | bytes 772
  3.1 0.7 copy-start.4
  5.0 49.3 %copy-start.8 = (bf16[128,128]{1,0:T(8,128)(2,1)S(1)}, bf16[128,128]{1,0:T(8,128)(2,1)}, u32[]{:S(2)}) copy-start(bf16[128,128]{1,0:T(8,128)(2,1)} %w_neigh_ref.1) | copy-start | bytes 98308
  5.0 49.3 %all-to-all-start = ((bf16[64,32,128]{2,1,0:T(8,128)(2,1)}), bf16[64,32,128]{2,1,0:T(8,128)(2,1)S(1)}, u32[]{:S(2)}, u32[]{:S(2)}) async-start(bf16[64,32,128]{2,1,0:T(8,128)(2,1)} %bitcast.4), calls=%async_computation | async-start | bytes 1048576 | tf_op jit(solution)/shard_map/all_to_all | solution.py:257
  24.2 30.0 %copy-start.5 = (bf16[64,128]{1,0:T(8,128)(2,1)S(1)}, bf16[64,128]{1,0:T(8,128)(2,1)}, u32[]{:S(2)}) copy-start(bf16[64,128]{1,0:T(8,128)(2,1)} %features_ref.3) | copy-start | bytes 49156
  24.2 30.0 %copy-start.7 = (bf16[128,128]{1,0:T(8,128)(2,1)S(1)}, bf16[128,128]{1,0:T(8,128)(2,1)}, u32[]{:S(2)}) copy-start(bf16[128,128]{1,0:T(8,128)(2,1)} %w_self_ref.1) | copy-start | bytes 98308
  24.3 30.0 %copy-start.12 = (f32[128]{0:T(128)S(1)}, f32[128]{0:T(128)}, u32[]{:S(2)}) copy-start(f32[128]{0:T(128)} %param.20) | copy-start | bytes 1540
  25.1 1.6 copy-start.3
  31.2 3.2 %copy-start = (bf16[1024,4096]{1,0:T(8,128)(2,1)}, bf16[1024,4096]{1,0:T(8,128)(2,1)S(1)}, u32[]{:S(2)}) copy-start(bf16[1024,4096]{1,0:T(8,128)(2,1)S(1)} %get-tuple-element.10.panel_hbm) | copy-start | bytes 25165828
  94.6 3.4 %copy-start.1 = (bf16[1024,4096]{1,0:T(8,128)(2,1)S(1)}, bf16[1024,4096]{1,0:T(8,128)(2,1)}, u32[]{:S(2)}) copy-start(bf16[1024,4096]{1,0:T(8,128)(2,1)} %copy-done) | copy-start | bytes 25165828
  98.0 64.3 %copy-start.2 = (bf16[1024,4096]{1,0:T(8,128)(2,1)S(1)}, bf16[1024,4096]{1,0:T(8,128)(2,1)}, u32[]{:S(2)}) copy-start(bf16[1024,4096]{1,0:T(8,128)(2,1)} %copy-done) | copy-start | bytes 25165828
  224.9 25.3 %copy-start.6 = (bf16[128,256]{1,0:T(8,128)(2,1)S(1)}, bf16[128,256]{1,0:T(8,128)(2,1)}, u32[]{:S(2)}) copy-start(bf16[128,256]{1,0:T(8,128)(2,1)} %w_ref.1) | copy-start | bytes 196612
  224.9 25.3 %copy-start.9 = (f32[256]{0:T(256)S(1)}, f32[256]{0:T(256)}, u32[]{:S(2)}) copy-start(f32[256]{0:T(256)} %param.22) | copy-start | bytes 3076

commit v2 on v1

--- a/solution.py
+++ b/solution.py
@@ -44,37 +44,62 @@
     return hi, (x - hi.astype(f32)).astype(bf16)
 
 
+def lane_sums(x):
+    ones = jnp.ones((8, x.shape[1]), bf16)
+    hi, rest = x.astype(bf16), x - x.astype(bf16).astype(f32)
+    mid, lo = split(rest)
+    over = ((1,), (1,))
+    return (dot(ones, lo, over) + dot(ones, mid, over)) + dot(ones, hi, over)
+
+
 def encode(z, s, dangling, out_ref):
     nodes = z.shape[0]
     top = jnp.max(jnp.abs(z), axis=0, keepdims=True)
     dsum = jnp.sum(z * dangling[:nodes], axis=0, keepdims=True)
     ssum = jnp.sum(s * dangling[nodes : nodes + 1], axis=1, keepdims=True)
     row = lax.broadcasted_iota(i32, (8, z.shape[1]), 0)
-    extra = jnp.where(row == 0, top, 0.0)
-    extra = jnp.where(row == 1, s, extra)
-    extra = jnp.where(row == 2, dsum, extra)
-    extra = jnp.where(row == 3, ssum, extra)
+    extra = jnp.where((row & 3) == 0, top, 0.0)
+    extra = jnp.where((row & 3) == 1, s, extra)
+    extra = jnp.where((row & 3) == 2, dsum, extra)
+    extra = jnp.where((row & 3) == 3, ssum, extra)
     level = jnp.ceil(jnp.log2(jnp.maximum(jnp.abs(extra), TINY)) * 256.0)
     level = jnp.minimum(level, TOP)
     gain = TOP * jnp.exp2(level * (-1.0 / 256.0))
-    codes = jnp.clip(jnp.round(z * gain[0:1]), -TOP, TOP).astype(i32)
-    extra_codes = jnp.clip(jnp.round(extra * gain), -TOP, TOP).astype(i32)
-    packed = jnp.concatenate([codes, level.astype(i32), extra_codes], axis=0).astype(i16)
+    codes = jnp.clip(jnp.round(z * gain[0:1]), -TOP, TOP)
+    extra_codes = jnp.clip(jnp.round(extra * gain), -TOP, TOP)
+    tail = jnp.where(row < 4, level, extra_codes)
+    packed = jnp.concatenate([codes, tail], axis=0).astype(i32).astype(i16)
     for k in range(out_ref.shape[0]):
         out_ref[k] = packed
 
 
-def pick_kernel(index_ref, features_ref, out_ref):
+def pick_kernel(count_ref, index_ref, features_ref, out_ref):
     features = features_ref[...]
     nodes = features.shape[0]
+    capacity = out_ref.shape[0] // count_ref.shape[0]
+    per_row = 128 // capacity
+    lane = lax.broadcasted_iota(i32, (1, 128), 1)
+    row = lax.broadcasted_iota(i32, (nodes, 128), 0)
     for k in range(index_ref.shape[0]):
-        row = lax.broadcasted_iota(i32, (nodes, 128), 0)
-        chosen = (row == index_ref[k : k + 1, :]).astype(f32).astype(bf16)
+        end = count_ref[k * per_row]
+        for m in range(1, per_row):
+            end = jnp.where(lane >= m * capacity, count_ref[k * per_row + m] + m * capacity, end)
+        index = jnp.where(lane < end, index_ref[k : k + 1, :], -1)
+        chosen = (row == index).astype(f32).astype(bf16)
         out_ref[pl.ds(k * 128, 128), :] = dot(chosen, features, ((0,), (0,))).astype(bf16)
 
 
 def panel_kernel(
-    rows_ref, cols_ref, count_ref, tiles_ref, neighbors_ref, panel_ref, own_ref, far_ref, total
+    rows_ref,
+    cols_ref,
+    count_ref,
+    tiles_ref,
+    neighbors_ref,
+    panel_ref,
+    sums_ref,
+    own_ref,
+    far_ref,
+    total,
 ):
     row_tiles = panel_ref.shape[0] // 256
     col_tiles = panel_ref.shape[1] // 128
@@ -92,6 +117,12 @@
         return 0
 
     lax.fori_loop(0, count_ref[0], place, 0)
+
+    for r in range(row_tiles):
+        whole = total[r * col_tiles]
+        for c in range(1, col_tiles):
+            whole = whole + total[r * col_tiles + c]
+        sums_ref[:, pl.ds(r * 128, 128)] = lane_sums(whole)
 
     def store(r, _):
         for c in range(col_tiles):
@@ -142,19 +173,9 @@
     encode(hidden, jnp.ones((1, hidden.shape[1]), f32), dangling_ref[...], out_ref)
 
 
-def spread_kernel(
-    node_total, parts, panel_hbm, packed_ref, out_ref, panel, z_parts, s_parts, sems
-):
+def spread_kernel(node_total, parts, first, panel_ref, sums_ref, packed_ref, out_ref, z_parts, s_row):
     zh, zl, nx = parts
-    half = panel.shape[0] // 2
-    loads = [
-        pltpu.make_async_copy(
-            panel_hbm.at[pl.ds(k * half, half)], panel.at[pl.ds(k * half, half)], sems.at[k]
-        )
-        for k in range(2)
-    ]
-    for load in loads:
-        load.start()
+    half = panel_ref.shape[0] // 2
     nodes = 64
     d_all = jnp.zeros((1, 128), f32)
     ds_all = jnp.zeros((1, 128), f32)
@@ -163,35 +184,37 @@
     for a in range(zh * zl * nx):
         h, m, x = a // (zl * nx), (a // nx) % zl, a % nx
         codes = packed_ref[x, m, h].astype(i32).astype(f32)
-        step = jnp.exp2(codes[nodes : nodes + 8] * (1.0 / 256.0)) * (1.0 / TOP)
+        tail = codes[nodes:]
+        step = jnp.exp2(tail * (1.0 / 256.0)) * (1.0 / TOP)
         hi, lo = split(codes[:nodes] * step[0:1])
         z_parts[pl.ds(a * nodes, nodes), pl.ds(0, 128)] = hi
         z_parts[pl.ds(a * nodes, nodes), pl.ds(128, 128)] = lo
-        extra = codes[nodes + 8 : nodes + 16] * step
+        extra = pltpu.roll(tail, 4, 0) * step
         d_all = d_all + extra[2:3]
         ds_all = ds_all + extra[3:4]
-        if a % 2:
-            hi, lo = split(jnp.where(lane < nodes, before, extra[1:2]))
-            s_parts[:, pl.ds((a // 2) * 128, 128)] = jnp.concatenate(
-                [hi.astype(f32), lo.astype(f32), jnp.zeros((14, 128), f32)], axis=0
-            ).astype(bf16)
+        if a % 2 and not first:
+            s_row[0:1, pl.ds((a // 2) * 128, 128)] = jnp.where(lane < nodes, before, extra[1:2])
         before = extra[1:2]
     d_all = d_all * (1.0 / node_total)
     ds_all = ds_all * (1.0 / node_total)
-    loads[0].wait()
-    first = dot(panel[:half], z_parts[...])
-    loads[1].wait()
-    second = dot(panel[half:], z_parts[...])
-    z_sum = (first[:, :128] + first[:, 128:]) + (second[:, :128] + second[:, 128:]) + d_all
-    s_sum = dot(s_parts[...], panel[...], ((1,), (1,)))
-    s_sum = (s_sum[0:1] + s_sum[1:2])
-    s_sum = s_sum[:, :half] + s_sum[:, half:]
+    upper = dot(panel_ref[:half], z_parts[...])
+    lower = dot(panel_ref[half:], z_parts[...])
+    z_sum = (upper[:, :128] + upper[:, 128:]) + (lower[:, :128] + lower[:, 128:]) + d_all
+    if first:
+        s_sum = sums_ref[...]
+    else:
+        part = jnp.zeros((half, 128), f32)
+        for c in range(panel_ref.shape[1] // 128):
+            at = pl.ds(c * 128, 128)
+            tile = panel_ref[:half, at].astype(f32) + panel_ref[half:, at].astype(f32)
+            part = part + tile * s_row[0:1, at]
+        s_sum = lane_sums(part)
     for b in range(half // nodes):
         out_ref[b, pl.ds(0, nodes), :] = z_sum[b * nodes : (b + 1) * nodes]
         two = s_sum[:, (b // 2) * 128 : (b // 2) * 128 + 128]
         if b % 2:
             two = pltpu.roll(two, nodes, 1)
-        out_ref[b, pl.ds(nodes, 8), :] = jnp.broadcast_to(two + ds_all, (8, 128))
+        out_ref[b, pl.ds(nodes, 8), :] = two + ds_all
 
 
 def gather_step(received_ref, hidden_ref):
@@ -251,23 +274,16 @@
     node_total = row_total * wide
     degree = neighbors.shape[1]
 
-    used = jnp.arange(capacity)[None, :] < send_count[0, 0][:, None]
-    index = jnp.where(used, send_rows[0, 0], -1).reshape(slots // 128, 128)
-    outgoing = call(pick_kernel, shape((slots, width), bf16), 2)(index, features)
-    received = lax.all_to_all(
-        outgoing.reshape(wide, capacity, width),
-        ("zh", "zl", "x"),
-        split_axis=0,
-        concat_axis=0,
-        tiled=True,
-    ).reshape(slots, width)
-
     smem = pl.BlockSpec(memory_space=pltpu.SMEM)
     vmem = pl.BlockSpec(memory_space=pltpu.VMEM)
-    panel, own, far = call(
+    outgoing = call(
+        pick_kernel, shape((slots, width), bf16), 3, in_specs=[smem, vmem, vmem], limit=8 << 20
+    )(send_count[0, 0], send_rows[0, 0].reshape(slots // 128, 128), features)
+    panel, row_sums, own, far = call(
         panel_kernel,
         [
             shape((2 * row_total, col_total), bf16),
+            shape((8, row_total), f32),
             shape((nodes, nodes), bf16),
             shape((nodes, slots), bf16),
         ],
@@ -276,7 +292,7 @@
         scratch=[pltpu.VMEM((row_total * col_total // (128 * 128), 128, 128), f32)],
         flops=1 << 24,
         nbytes=20 << 20,
-        limit=28 << 20,
+        limit=14 << 20,
     )(tile_rows[0, 0], tile_cols[0, 0], tile_count[0], tiles[0, 0], neighbors)
 
     mark = dangling.astype(f32)
@@ -288,27 +304,36 @@
         axis=0,
     )
 
-    packed_shape = shape((zh, nodes + 16, width), i16)
+    outgoing, panel, row_sums, own, far, marks = lax.optimization_barrier(
+        (outgoing, panel, row_sums, own, far, marks)
+    )
+    received = lax.all_to_all(
+        outgoing.reshape(wide, capacity, width),
+        ("zh", "zl", "x"),
+        split_axis=0,
+        concat_axis=0,
+        tiled=True,
+    ).reshape(slots, width)
+
+    packed_shape = shape((zh, nodes + 8, width), i16)
     hidden, packed = call(
         functools.partial(hidden_kernel, degree),
         [shape((nodes, width), f32), packed_shape],
         8,
+        limit=8 << 20,
     )(features, received, own, far, w_self, w_neigh, bias_hidden[None, :], marks)
 
-    spread = call(
-        functools.partial(spread_kernel, node_total, (zh, zl, nx)),
-        shape((narrow, nodes + 8, width), f32),
-        2,
-        in_specs=[pl.BlockSpec(memory_space=pl.ANY), vmem],
-        scratch=[
-            pltpu.VMEM((2 * row_total, col_total), bf16),
-            pltpu.VMEM((col_total, 2 * width), bf16),
-            pltpu.VMEM((16, col_total), bf16),
-            pltpu.SemaphoreType.DMA((2,)),
-        ],
-        flops=2 * 2 * row_total * col_total * 256,
-        nbytes=10 << 20,
-    )
+    def spread(packed, repeat):
+        return call(
+            functools.partial(spread_kernel, node_total, (zh, zl, nx), repeat == 0),
+            shape((narrow, nodes + 8, width), f32),
+            3,
+            scratch=[pltpu.VMEM((col_total, 2 * width), bf16), pltpu.VMEM((8, col_total), f32)],
+            flops=2 * 2 * row_total * col_total * 256,
+            nbytes=10 << 20,
+            limit=12 << 20,
+        )(panel, row_sums, packed)
+
     for repeat in range(ITERS):
         got = lax.all_to_all(packed, "zh", split_axis=0, concat_axis=0, tiled=True)
         got = lax.all_to_all(
@@ -319,11 +344,11 @@
             tiled=True,
         )
         got = lax.all_gather(got, "x", axis=0)
-        partial = spread(panel, got)
+        partial = spread(got, repeat)
         sums = lax.all_to_all(partial, "narrow", split_axis=0, concat_axis=0, tiled=True)
         if repeat < ITERS - 1:
-            packed = call(step_kernel, packed_shape, 3)(sums, hidden, marks)
-    return call(last_kernel, shape((nodes, w_out.shape[1]), f32), 4)(
+            packed = call(step_kernel, packed_shape, 3, limit=4 << 20)(sums, hidden, marks)
+    return call(last_kernel, shape((nodes, w_out.shape[1]), f32), 4, limit=4 << 20)(
         sums, hidden, w_out, bias_out[None, :]
     )
 

time: 252 us -> 240 us (0.952)
  blocking collectives: 168 us -> 213 us
  waiting for transfers between devices: 19.7 us -> 0 us
  starting transfers between devices: 19.2 us -> 0 us
  Pallas kernels: 31.3 us -> 18.8 us
  local copies, waits for them, and re-layouts: 10.9 us -> 6.08 us
    all_to_all x0 -> x1, blocking collectives: none -> 49.7 us  [body(): lax.all_to_all(outgoing.reshape(wide, capacity, width), ('zh', 'zl', 'x')...]
    all_to_all x1 -> x0, waiting for transfers between devices: 19.7 us -> none  [body(): lax.all_to_all(outgoing.reshape(wide, capacity, width), ('zh', 'zl', 'x')...]
    all_to_all x1 -> x0, starting transfers between devices: 19.2 us -> none  [body(): lax.all_to_all(outgoing.reshape(wide, capacity, width), ('zh', 'zl', 'x')...]
    pallas_call x8, Pallas kernels: 30.8 us -> 18.4 us  [the longest x3 11.2 us: spread(): call(functools.partial(spread_kernel, node_total, (zh, zl, nx), repeat ==...]
    unnamed x33 -> x22, local copies, waits for them, and re-layouts: 10.4 us -> 5.88 us
  transfers between devices with their start and end apart: 1 -> 0, of which waited for: 1 -> 0; matrix products, arithmetic and copies ran while one was open for 0% -> 0% of each run, Pallas kernels for 2% -> 0%
where the time goes in v2:
time: 240 us; the launch traced here: 239 us
  blocking collectives  213 us (89%)
  Pallas kernels  18.8 us (8%)
  local copies, waits for them, and re-layouts  6.08 us (3%)
    all_to_all x3, blocking collectives, body(): lax.all_to_all(partial, 'narrow', split_axis=0, concat_axis=0, tiled=True)  51.7 us
    all_to_all x1, blocking collectives, body(): lax.all_to_all(outgoing.reshape(wide, capacity, width), ('zh', 'zl', 'x')...  49.7 us
    all_to_all x3, blocking collectives, body(): got = lax.all_to_all(packed, 'zh', split_axis=0, concat_axis=0, tiled=True)  45.7 us
    all_gather x3, blocking collectives, body(): got = lax.all_gather(got, 'x', axis=0)  37 us
    all_to_all x3, blocking collectives, body(): lax.all_to_all(jnp.broadcast_to(got[None], (zl,) + got.shape), 'zl', spli...  28.5 us
    pallas_call x3, Pallas kernels, spread(): call(functools.partial(spread_kernel, node_total, (zh, zl, nx), repeat ==...  11.2 us
    unnamed x22, local copies, waits for them, and re-layouts  5.88 us
    pallas_call x1, Pallas kernels, body(): call(panel_kernel, [shape((2 * row_total, col_total), bf16), shape((8, ro...  5.15 us

profile of v2, /device:TPU:1, one launch (start us, length us, event | category | flops | bytes accessed | tf_op | source)
XLA Modules:
  0.0 239.1 jit_solution(16568717407478800961)
XLA Ops:
  0.7 0.7 convert_element_type.5
  1.3 0.8 copy.19
  2.1 0.1 reshape_squeeze.3.index_ref
  2.2 0.8 copy.20.neighbors_ref
  3.0 0.1 pad_maximum_fusion.dangling_ref
  3.1 0.0 copy-start.1
  3.1 0.7 copy-done.1
  3.8 0.0 copy-start.6
  3.8 0.7 copy-done.6
  4.4 0.9 shard_map.136
  5.3 0.0 copy-start
  5.3 1.6 copy-done
  6.9 0.0 copy-start.7
  6.9 0.7 copy-done.7
  7.6 0.0 copy-start.8
  7.6 0.7 copy-done.8
  8.2 0.0 copy-start.3
  8.2 0.0 copy-start.4
  8.2 0.0 copy-start.9
  8.2 5.2 %shard_map.137 = (bf16[1024,4096]{1,0:T(8,128)(2,1)S(1)}, f32[8,512]{1,0:T(8,128)S(1)}, bf16[64,64]{1,0:T(8,128)(2,1)S(1)}, bf16[64,2048]{1,0:T(8,128)(2,1)S(1)}) custom-call(s32[64]{0:T(128)S(1)} %bitcast.23, s32[64]{0:T(128)S(1)} %bitcast.24, s32[1]{0:T(128)} %bitcast.14.count_ref, bf16[64,128,128]{2,1,0:T(8,128)(2,1)S(1)} %bitcast.18, ...), custom_call_target="tpu_custom_call" | custom-call | flops 16777216 | bytes 20971520 | tf_op jit(solution)/shard_map/pallas_call | solution.py:282
  13.4 49.7 %all_to_all.50 = bf16[64,32,128]{2,1,0:T(8,128)(2,1)S(1)} all-to-all(bf16[64,32,128]{2,1,0:T(8,128)(2,1)S(1)} %bitcast.19), channel_id=1, replica_groups=mesh['zh'=4,'zl'=4,'x'=4,'narrow'=8] {'zh','zl','x'}, dimensions={0} | all-to-all | bytes 1048576 | tf_op jit(solution)/shard_map/all_to_all | solution.py:310
  63.2 0.0 copy-done.3
  63.2 0.0 copy-done.4
  63.2 0.0 copy-done.9
  63.2 0.4 shard_map.138
  63.6 16.4 %all_to_all.51 = s16[4,72,128]{2,1,0:T(8,128)(2,1)S(1)} all-to-all(s16[4,72,128]{2,1,0:T(8,128)(2,1)S(1)} %get-tuple-element.27), channel_id=1, replica_groups=mesh['zh'=4,'zl'=4,'x'=4,'narrow'=8] {'zh'}, dimensions={0} | all-to-all | bytes 147456 | tf_op jit(solution)/shard_map/all_to_all | solution.py:338
  80.0 10.1 %all_to_all.52 = s16[4,4,72,128]{3,2,1,0:T(8,128)(2,1)S(1)} all-to-all(s16[4,4,72,128]{3,2,1,0:T(8,128)(2,1)S(1)} %broadcast_in_dim.17), channel_id=1, replica_groups=mesh['zh'=4,'zl'=4,'x'=4,'narrow'=8] {'zl'}, dimensions={0} | all-to-all | bytes 589824 | tf_op jit(solution)/shard_map/all_to_all | solution.py:339
  90.1 12.9 %all-gather.6 = s16[16,4,72,128]{3,2,1,0:T(8,128)(2,1)S(1)} all-gather(s16[4,4,72,128]{3,2,1,0:T(8,128)(2,1)S(1)} %all_to_all.52), channel_id=2, replica_groups=mesh['zh'=4,'zl'=4,'x'=4,'narrow'=8] {'x'}, dimensions={0}, use_global_device_ids=true | all-gather | bytes 1474560 | tf_op jit(solution)/shard_map/all_gather | solution.py:346
  103.1 2.7 %shard_map.139 = f32[8,72,128]{2,1,0:T(8,128)S(1)} custom-call(bf16[1024,4096]{1,0:T(8,128)(2,1)S(1)} %get-tuple-element.21.panel_ref, f32[8,512]{1,0:T(8,128)S(1)} %get-tuple-element.22.sums_ref, s16[4,4,4,72,128]{4,3,2,1,0:T(8,128)(2,1)S(1)} %bitcast.16), custom_call_target="tpu_custom_call" | custom-call | flops 2147483648 | bytes 10485760 | tf_op jit(solution)/shard_map/pallas_call | solution.py:327
  105.8 18.4 %all_to_all.53.received_ref = f32[8,72,128]{2,1,0:T(8,128)S(1)} all-to-all(f32[8,72,128]{2,1,0:T(8,128)S(1)} %shard_map.139), channel_id=1, replica_groups=mesh['zh'=4,'zl'=4,'x'=4,'narrow'=8] {'narrow'}, dimensions={0} | all-to-all | bytes 589824 | tf_op jit(solution)/shard_map/all_to_all | solution.py:348
  124.1 0.2 shard_map.140
  124.3 14.5 %all_to_all.54 = s16[4,72,128]{2,1,0:T(8,128)(2,1)S(1)} all-to-all(s16[4,72,128]{2,1,0:T(8,128)(2,1)S(1)} %shard_map.140), channel_id=1, replica_groups=mesh['zh'=4,'zl'=4,'x'=4,'narrow'=8] {'zh'}, dimensions={0} | all-to-all | bytes 147456 | tf_op jit(solution)/shard_map/all_to_all | solution.py:338
  138.9 9.3 %all_to_all.55 = s16[4,4,72,128]{3,2,1,0:T(8,128)(2,1)S(1)} all-to-all(s16[4,4,72,128]{3,2,1,0:T(8,128)(2,1)S(1)} %broadcast_in_dim.18), channel_id=1, replica_groups=mesh['zh'=4,'zl'=4,'x'=4,'narrow'=8] {'zl'}, dimensions={0} | all-to-all | bytes 589824 | tf_op jit(solution)/shard_map/all_to_all | solution.py:339
  148.2 12.0 %all-gather.7 = s16[16,4,72,128]{3,2,1,0:T(8,128)(2,1)S(1)} all-gather(s16[4,4,72,128]{3,2,1,0:T(8,128)(2,1)S(1)} %all_to_all.55), channel_id=3, replica_groups=mesh['zh'=4,'zl'=4,'x'=4,'narrow'=8] {'x'}, dimensions={0}, use_global_device_ids=true | all-gather | bytes 1474560 | tf_op jit(solution)/shard_map/all_gather | solution.py:346
  160.2 4.3 %shard_map.141 = f32[8,72,128]{2,1,0:T(8,128)S(1)} custom-call(bf16[1024,4096]{1,0:T(8,128)(2,1)S(1)} %get-tuple-element.21.panel_ref, f32[8,512]{1,0:T(8,128)S(1)} %get-tuple-element.22.sums_ref, s16[4,4,4,72,128]{4,3,2,1,0:T(8,128)(2,1)S(1)} %bitcast.17), custom_call_target="tpu_custom_call" | custom-call | flops 2147483648 | bytes 10485760 | tf_op jit(solution)/shard_map/pallas_call | solution.py:327
  164.5 16.7 %all_to_all.56.received_ref = f32[8,72,128]{2,1,0:T(8,128)S(1)} all-to-all(f32[8,72,128]{2,1,0:T(8,128)S(1)} %shard_map.141), channel_id=1, replica_groups=mesh['zh'=4,'zl'=4,'x'=4,'narrow'=8] {'narrow'}, dimensions={0} | all-to-all | bytes 589824 | tf_op jit(solution)/shard_map/all_to_all | solution.py:348
  181.2 0.2 shard_map.142
  181.4 14.8 %all_to_all.57 = s16[4,72,128]{2,1,0:T(8,128)(2,1)S(1)} all-to-all(s16[4,72,128]{2,1,0:T(8,128)(2,1)S(1)} %shard_map.142), channel_id=1, replica_groups=mesh['zh'=4,'zl'=4,'x'=4,'narrow'=8] {'zh'}, dimensions={0} | all-to-all | bytes 147456 | tf_op jit(solution)/shard_map/all_to_all | solution.py:338
  196.3 9.0 %all_to_all.58 = s16[4,4,72,128]{3,2,1,0:T(8,128)(2,1)S(1)} all-to-all(s16[4,4,72,128]{3,2,1,0:T(8,128)(2,1)S(1)} %broadcast_in_dim.19), channel_id=1, replica_groups=mesh['zh'=4,'zl'=4,'x'=4,'narrow'=8] {'zl'}, dimensions={0} | all-to-all | bytes 589824 | tf_op jit(solution)/shard_map/all_to_all | solution.py:339
  205.3 12.1 %all-gather.8 = s16[16,4,72,128]{3,2,1,0:T(8,128)(2,1)S(1)} all-gather(s16[4,4,72,128]{3,2,1,0:T(8,128)(2,1)S(1)} %all_to_all.58), channel_id=4, replica_groups=mesh['zh'=4,'zl'=4,'x'=4,'narrow'=8] {'x'}, dimensions={0}, use_global_device_ids=true | all-gather | bytes 1474560 | tf_op jit(solution)/shard_map/all_gather | solution.py:346
  217.3 0.0 copy-start.2
  217.3 0.0 copy-start.5
  217.3 4.2 %shard_map.143 = f32[8,72,128]{2,1,0:T(8,128)S(1)} custom-call(bf16[1024,4096]{1,0:T(8,128)(2,1)S(1)} %get-tuple-element.21.panel_ref, f32[8,512]{1,0:T(8,128)S(1)} %get-tuple-element.22.sums_ref, s16[4,4,4,72,128]{4,3,2,1,0:T(8,128)(2,1)S(1)} %bitcast.15), custom_call_target="tpu_custom_call" | custom-call | flops 2147483648 | bytes 10485760 | tf_op jit(solution)/shard_map/pallas_call | solution.py:327
  221.6 16.7 %all_to_all.59.received_ref = f32[8,72,128]{2,1,0:T(8,128)S(1)} all-to-all(f32[8,72,128]{2,1,0:T(8,128)S(1)} %shard_map.143), channel_id=1, replica_groups=mesh['zh'=4,'zl'=4,'x'=4,'narrow'=8] {'narrow'}, dimensions={0} | all-to-all | bytes 589824 | tf_op jit(solution)/shard_map/all_to_all | solution.py:348
  238.3 0.0 copy-done.2
  238.3 0.0 copy-done.5
  238.3 0.8 shard_map.144
  (6 shorter events, 0.1 us)
Async XLA Ops:
  3.1 0.7 copy-start.1
  3.8 0.7 copy-start.6
  5.3 1.6 copy-start
  6.9 0.7 copy-start.7
  7.6 0.7 copy-start.8
  8.2 54.9 %copy-start.3 = (bf16[128,128]{1,0:T(8,128)(2,1)S(1)}, bf16[128,128]{1,0:T(8,128)(2,1)}, u32[]{:S(2)}) copy-start(bf16[128,128]{1,0:T(8,128)(2,1)} %w_self_ref.1) | copy-start | bytes 98308
  8.2 54.9 %copy-start.4 = (bf16[128,128]{1,0:T(8,128)(2,1)S(1)}, bf16[128,128]{1,0:T(8,128)(2,1)}, u32[]{:S(2)}) copy-start(bf16[128,128]{1,0:T(8,128)(2,1)} %w_neigh_ref.1) | copy-start | bytes 98308
  8.2 54.9 %copy-start.9 = (f32[128]{0:T(128)S(1)}, f32[128]{0:T(128)}, u32[]{:S(2)}) copy-start(f32[128]{0:T(128)} %param.20) | copy-start | bytes 1540
  217.3 20.9 %copy-start.2 = (bf16[128,256]{1,0:T(8,128)(2,1)S(1)}, bf16[128,256]{1,0:T(8,128)(2,1)}, u32[]{:S(2)}) copy-start(bf16[128,256]{1,0:T(8,128)(2,1)} %w_ref.1) | copy-start | bytes 196612
  217.3 20.9 %copy-start.5 = (f32[256]{0:T(256)S(1)}, f32[256]{0:T(256)}, u32[]{:S(2)}) copy-start(f32[256]{0:T(256)} %param.22) | copy-start | bytes 3076

commit v3 on v2

--- a/solution.py
+++ b/solution.py
@@ -73,34 +73,50 @@
         out_ref[k] = packed
 
 
-def pick_kernel(count_ref, index_ref, features_ref, out_ref):
-    features = features_ref[...]
-    nodes = features.shape[0]
-    capacity = out_ref.shape[0] // count_ref.shape[0]
-    per_row = 128 // capacity
-    lane = lax.broadcasted_iota(i32, (1, 128), 1)
-    row = lax.broadcasted_iota(i32, (nodes, 128), 0)
-    for k in range(index_ref.shape[0]):
-        end = count_ref[k * per_row]
-        for m in range(1, per_row):
-            end = jnp.where(lane >= m * capacity, count_ref[k * per_row + m] + m * capacity, end)
-        index = jnp.where(lane < end, index_ref[k : k + 1, :], -1)
-        chosen = (row == index).astype(f32).astype(bf16)
-        out_ref[pl.ds(k * 128, 128), :] = dot(chosen, features, ((0,), (0,))).astype(bf16)
-
-
-def panel_kernel(
-    rows_ref,
-    cols_ref,
-    count_ref,
-    tiles_ref,
-    neighbors_ref,
+def head_kernel(
+    count_hbm,
+    send_hbm,
+    features_hbm,
+    rows_hbm,
+    cols_hbm,
+    used_hbm,
+    tiles_hbm,
+    linked_hbm,
+    dangling_hbm,
+    outgoing_ref,
     panel_ref,
     sums_ref,
     own_ref,
     far_ref,
+    marks_ref,
+    count_ref,
+    send_ref,
+    features_ref,
+    rows_ref,
+    cols_ref,
+    used_ref,
+    tiles_ref,
+    linked_ref,
+    dangling_ref,
+    index_ref,
     total,
+    sems,
 ):
+    pairs = (
+        (count_hbm, count_ref),
+        (send_hbm, send_ref),
+        (features_hbm, features_ref),
+        (linked_hbm, linked_ref),
+        (dangling_hbm, dangling_ref),
+        (rows_hbm, rows_ref),
+        (cols_hbm, cols_ref),
+        (used_hbm, used_ref),
+        (tiles_hbm, tiles_ref),
+    )
+    loads = [pltpu.make_async_copy(a, b, sems.at[k]) for k, (a, b) in enumerate(pairs)]
+    for load in loads:
+        load.start()
+
     row_tiles = panel_ref.shape[0] // 256
     col_tiles = panel_ref.shape[1] // 128
     zero = jnp.zeros((128, 128), f32)
@@ -110,45 +126,78 @@
         return 0
 
     lax.fori_loop(0, row_tiles * col_tiles, clear, 0)
-
-    def place(t, _):
-        p = rows_ref[t] * col_tiles + cols_ref[t]
-        total[p] = total[p] + tiles_ref[t].astype(f32)
-        return 0
-
-    lax.fori_loop(0, count_ref[0], place, 0)
-
-    for r in range(row_tiles):
-        whole = total[r * col_tiles]
-        for c in range(1, col_tiles):
-            whole = whole + total[r * col_tiles + c]
-        sums_ref[:, pl.ds(r * 128, 128)] = lane_sums(whole)
-
-    def store(r, _):
-        for c in range(col_tiles):
-            hi, lo = split(total[r * col_tiles + c])
-            panel_ref[pl.ds(pl.multiple_of(r * 128, 128), 128), pl.ds(c * 128, 128)] = hi
-            panel_ref[
-                pl.ds(pl.multiple_of((r + row_tiles) * 128, 128), 128), pl.ds(c * 128, 128)
-            ] = lo
-        return 0
-
-    lax.fori_loop(0, row_tiles, store, 0)
-
-    nodes = own_ref.shape[0]
-    degree = neighbors_ref.shape[1]
-    linked = neighbors_ref[...]
+    for load in loads[:5]:
+        load.wait()
+
+    features = features_ref[...]
+    nodes = features.shape[0]
+    lists, capacity = send_ref.shape
+    per_row = 128 // capacity
+    lane = lax.broadcasted_iota(i32, (1, 128), 1)
+    row = lax.broadcasted_iota(i32, (nodes, 128), 0)
+    for m in range(per_row):
+        index_ref[:, pl.ds(m * capacity, capacity)] = send_ref[
+            pl.ds(m, lists // per_row, stride=per_row), :
+        ]
+    for k in range(lists // per_row):
+        end = count_ref[0, k * per_row]
+        for m in range(1, per_row):
+            end = jnp.where(lane >= m * capacity, count_ref[0, k * per_row + m] + m * capacity, end)
+        index = jnp.where(lane < end, index_ref[k : k + 1, :], -1)
+        chosen = (row == index).astype(f32).astype(bf16)
+        outgoing_ref[pl.ds(k * 128, 128), :] = dot(chosen, features, ((0,), (0,))).astype(bf16)
+
+    same = lax.broadcasted_iota(i32, (nodes, nodes), 0) == lax.broadcasted_iota(
+        i32, (nodes, nodes), 1
+    )
+    eye = same.astype(f32).astype(bf16)
+    linked = linked_ref[...]
+    high = linked >> 6
+    over = ((1,), (1,))
+    linked = 64.0 * dot(eye, high.astype(f32).astype(bf16), over) + dot(
+        eye, (linked - (high << 6)).astype(f32).astype(bf16), over
+    )
+    linked = linked.astype(i32)
 
     def counts(width, offset):
         slot = lax.broadcasted_iota(i32, (nodes, width), 1) + offset
         got = jnp.zeros((nodes, width), f32)
-        for k in range(degree):
+        for k in range(linked.shape[1]):
             got = got + jnp.where(linked[:, k : k + 1] == slot, 1.0, 0.0)
         return got.astype(bf16)
 
     own_ref[...] = counts(nodes, 0)
     for c in range(0, far_ref.shape[1], 256):
         far_ref[:, pl.ds(c, 256)] = counts(256, nodes + c)
+
+    mark = dangling_ref[...].astype(f32)
+    column = jnp.sum(jnp.where(same, jnp.broadcast_to(mark, same.shape), 0.0), axis=1, keepdims=True)
+    marks_ref[pl.ds(0, nodes), :] = jnp.broadcast_to(column, (nodes, 128))
+    marks_ref[pl.ds(nodes, 8), :] = jnp.zeros((8, 128), f32)
+    marks_ref[pl.ds(nodes, 8), pl.ds(0, nodes)] = jnp.broadcast_to(mark, (8, nodes))
+
+    for load in loads[5:]:
+        load.wait()
+
+    def place(t, _):
+        p = rows_ref[0, t] * col_tiles + cols_ref[0, t]
+        total[p] = total[p] + tiles_ref[t].astype(f32)
+        return 0
+
+    lax.fori_loop(0, used_ref[0, 0], place, 0)
+
+    def store(r, _):
+        at = pl.ds(pl.multiple_of(r * 128, 128), 128)
+        below = pl.ds(pl.multiple_of((r + row_tiles) * 128, 128), 128)
+        whole = jnp.zeros((128, 128), f32)
+        for c in range(col_tiles):
+            tile = total[r * col_tiles + c]
+            whole = whole + tile
+            panel_ref[at, pl.ds(c * 128, 128)], panel_ref[below, pl.ds(c * 128, 128)] = split(tile)
+        sums_ref[:, at] = lane_sums(whole)
+        return 0
+
+    lax.fori_loop(0, row_tiles, store, 0)
 
 
 def hidden_kernel(
@@ -183,7 +232,7 @@
     before = None
     for a in range(zh * zl * nx):
         h, m, x = a // (zl * nx), (a // nx) % zl, a % nx
-        codes = packed_ref[x, m, h].astype(i32).astype(f32)
+        codes = packed_ref[m, x, h].astype(i32).astype(f32)
         tail = codes[nodes:]
         step = jnp.exp2(tail * (1.0 / 256.0)) * (1.0 / TOP)
         hi, lo = split(codes[:nodes] * step[0:1])
@@ -274,38 +323,45 @@
     node_total = row_total * wide
     degree = neighbors.shape[1]
 
-    smem = pl.BlockSpec(memory_space=pltpu.SMEM)
-    vmem = pl.BlockSpec(memory_space=pltpu.VMEM)
-    outgoing = call(
-        pick_kernel, shape((slots, width), bf16), 3, in_specs=[smem, vmem, vmem], limit=8 << 20
-    )(send_count[0, 0], send_rows[0, 0].reshape(slots // 128, 128), features)
-    panel, row_sums, own, far = call(
-        panel_kernel,
+    outgoing, panel, row_sums, own, far, marks = call(
+        head_kernel,
         [
+            shape((slots, width), bf16),
             shape((2 * row_total, col_total), bf16),
             shape((8, row_total), f32),
             shape((nodes, nodes), bf16),
             shape((nodes, slots), bf16),
+            shape((nodes + 8, 128), f32),
         ],
-        5,
-        in_specs=[smem, smem, smem, vmem, vmem],
-        scratch=[pltpu.VMEM((row_total * col_total // (128 * 128), 128, 128), f32)],
+        9,
+        in_specs=[pl.BlockSpec(memory_space=pltpu.HBM)] * 9,
+        scratch=[
+            pltpu.SMEM((1, wide), i32),
+            pltpu.VMEM((wide, capacity), i32),
+            pltpu.VMEM((nodes, width), bf16),
+            pltpu.SMEM(tile_rows.shape[1:], i32),
+            pltpu.SMEM(tile_rows.shape[1:], i32),
+            pltpu.SMEM((1, 1), i32),
+            pltpu.VMEM(tiles.shape[2:], bf16),
+            pltpu.VMEM((degree, nodes), i32),
+            pltpu.VMEM((1, nodes), i32),
+            pltpu.VMEM((wide * capacity // 128, 128), i32),
+            pltpu.VMEM((row_total * col_total // (128 * 128), 128, 128), f32),
+            pltpu.SemaphoreType.DMA((9,)),
+        ],
         flops=1 << 24,
         nbytes=20 << 20,
-        limit=14 << 20,
-    )(tile_rows[0, 0], tile_cols[0, 0], tile_count[0], tiles[0, 0], neighbors)
-
-    mark = dangling.astype(f32)
-    marks = jnp.concatenate(
-        [
-            jnp.broadcast_to(mark[:, None], (nodes, 128)),
-            jnp.broadcast_to(jnp.pad(mark, (0, 128 - nodes))[None, :], (8, 128)),
-        ],
-        axis=0,
-    )
-
-    outgoing, panel, row_sums, own, far, marks = lax.optimization_barrier(
-        (outgoing, panel, row_sums, own, far, marks)
+        limit=16 << 20,
+    )(
+        send_count[0],
+        send_rows[0, 0],
+        features,
+        tile_rows[0],
+        tile_cols[0],
+        tile_count,
+        tiles[0, 0],
+        neighbors.T,
+        dangling[None, :],
     )
     received = lax.all_to_all(
         outgoing.reshape(wide, capacity, width),
@@ -336,14 +392,17 @@
 
     for repeat in range(ITERS):
         got = lax.all_to_all(packed, "zh", split_axis=0, concat_axis=0, tiled=True)
-        got = lax.all_to_all(
-            jnp.broadcast_to(got[None], (zl,) + got.shape),
-            "zl",
-            split_axis=0,
-            concat_axis=0,
-            tiled=True,
-        )
-        got = lax.all_gather(got, "x", axis=0)
+        if repeat == 1:
+            got = lax.all_gather(got, ("zl", "x"), axis=0)
+        else:
+            got = lax.all_to_all(
+                jnp.broadcast_to(got[None], (zl * nx,) + got.shape),
+                ("zl", "x"),
+                split_axis=0,
+                concat_axis=0,
+                tiled=True,
+            )
+        got = got.reshape((zl, nx) + got.shape[1:])
         partial = spread(got, repeat)
         sums = lax.all_to_all(partial, "narrow", split_axis=0, concat_axis=0, tiled=True)
         if repeat < ITERS - 1:
@@ -356,7 +415,7 @@
 def solution(mesh):
     wide, narrow = mesh.devices.shape
     nx = 4 if wide % 64 == 0 else 2
-    zl = 4 if wide % 64 == 0 else 2
+    zl = 2
     split_mesh = Mesh(
         mesh.devices.reshape(wide // (zl * nx), zl, nx, narrow), ("zh", "zl", "x", "narrow")
     )

time: 240 us -> 235 us (0.979)
  blocking collectives: 213 us -> 209 us
    all_gather x3 -> x1, blocking collectives: 37 us -> 25.5 us  [body(): got = lax.all_gather(got, ('zl', 'x'), axis=0)]
    all_to_all x3, blocking collectives: 45.7 us -> 52.2 us  [body(): got = lax.all_to_all(packed, 'zh', split_axis=0, concat_axis=0, tiled=True)]
    all_to_all x3 -> x2, blocking collectives: 28.5 us -> 31 us  [body(): lax.all_to_all(jnp.broadcast_to(got[None], (zl * nx,) + got.shape), ('zl'...]
    all_to_all x3, blocking collectives: 51.7 us -> 49.3 us  [body(): lax.all_to_all(partial, 'narrow', split_axis=0, concat_axis=0, tiled=True)]
    unnamed x22 -> x25, local copies, waits for them, and re-layouts: 5.88 us -> 6.44 us
    pallas_call x2 -> x1, Pallas kernels: 6.04 us -> 5.93 us  [body(): call(head_kernel, [shape((slots, width), bf16), shape((2 * row_total, col...]
where the time goes in v3:
time: 235 us
  blocking collectives  209 us (89%)
  Pallas kernels  18.7 us (8%)
  local copies, waits for them, and re-layouts  6.75 us (3%)
    all_to_all x3, blocking collectives, body(): got = lax.all_to_all(packed, 'zh', split_axis=0, concat_axis=0, tiled=True)  52.2 us
    all_to_all x1, blocking collectives, body(): lax.all_to_all(outgoing.reshape(wide, capacity, width), ('zh', 'zl', 'x')...  50.7 us
    all_to_all x3, blocking collectives, body(): lax.all_to_all(partial, 'narrow', split_axis=0, concat_axis=0, tiled=True)  49.3 us
    all_to_all x2, blocking collectives, body(): lax.all_to_all(jnp.broadcast_to(got[None], (zl * nx,) + got.shape), ('zl'...  31 us
    all_gather x1, blocking collectives, body(): got = lax.all_gather(got, ('zl', 'x'), axis=0)  25.5 us
    pallas_call x3, Pallas kernels, spread(): call(functools.partial(spread_kernel, node_total, (zh, zl, nx), repeat ==...  11.1 us
    unnamed x25, local copies, waits for them, and re-layouts  6.44 us
    pallas_call x1, Pallas kernels, body(): call(head_kernel, [shape((slots, width), bf16), shape((2 * row_total, col...  5.93 us

profile of v3, /device:TPU:1, one launch (start us, length us, event | category | flops | bytes accessed | tf_op | source)
XLA Modules:
  0.0 234.8 jit_solution(16483065433941843500)
XLA Ops:
  0.7 0.8 copy.16
  1.4 0.0 copy-start
  1.5 1.6 copy-done
  3.0 0.0 copy-start.1
  3.0 0.7 copy-done.1
  3.8 0.0 copy-start.5
  3.8 0.7 copy-done.5
  4.5 0.0 copy-start.8
  4.5 0.7 copy-done.8
  5.1 0.0 copy-start.9
  5.1 0.7 copy-done.9
  5.8 0.0 copy-start.10
  5.8 0.7 copy-done.10
  6.4 0.0 copy-start.11
  6.4 0.7 copy-done.11
  7.1 0.0 copy-start.3
  7.1 0.0 copy-start.4
  7.1 0.0 copy-start.7
  7.1 5.9 %shard_map.136 = (bf16[2048,128]{1,0:T(8,128)(2,1)S(1)}, bf16[1024,4096]{1,0:T(8,128)(2,1)S(1)}, f32[8,512]{1,0:T(8,128)S(1)}, bf16[64,64]{1,0:T(8,128)(2,1)S(1)...) custom-call(s32[1,64]{1,0:T(1,128)S(1)} %bitcast.24, s32[64,32]{1,0:T(8,128)S(1)} %bitcast.20, ...), custom_call_target="tpu_custom_call" | custom-call | flops 16777216 | bytes 20971520 | tf_op jit(solution)/shard_map/pallas_call | solution.py:326
  13.0 50.7 %all_to_all.45 = bf16[64,32,128]{2,1,0:T(8,128)(2,1)S(1)} all-to-all(bf16[64,32,128]{2,1,0:T(8,128)(2,1)S(1)} %bitcast.19), channel_id=1, replica_groups=mesh['zh'=8,'zl'=2,'x'=4,'narrow'=8] {'zh','zl','x'}, dimensions={0} | all-to-all | bytes 1048576 | tf_op jit(solution)/shard_map/all_to_all | solution.py:366
  63.7 0.0 copy-done.3
  63.7 0.0 copy-done.4
  63.7 0.0 copy-done.7
  63.7 0.4 shard_map.137
  64.1 18.3 %all_to_all.46 = s16[8,72,128]{2,1,0:T(8,128)(2,1)S(1)} all-to-all(s16[8,72,128]{2,1,0:T(8,128)(2,1)S(1)} %get-tuple-element.19), channel_id=1, replica_groups=mesh['zh'=8,'zl'=2,'x'=4,'narrow'=8] {'zh'}, dimensions={0} | all-to-all | bytes 294912 | tf_op jit(solution)/shard_map/all_to_all | solution.py:394
  82.4 0.2 broadcast_in_dim.23
  82.6 14.9 %all_to_all.47 = s16[8,8,72,128]{3,2,1,0:T(8,128)(2,1)S(1)} all-to-all(s16[8,8,72,128]{3,2,1,0:T(8,128)(2,1)S(1)} %broadcast_in_dim.23), channel_id=1, replica_groups=mesh['zh'=8,'zl'=2,'x'=4,'narrow'=8] {'zl','x'}, dimensions={0} | all-to-all | bytes 2359296 | tf_op jit(solution)/shard_map/all_to_all | solution.py:398
  97.5 2.7 %shard_map.138 = f32[8,72,128]{2,1,0:T(8,128)S(1)} custom-call(bf16[1024,4096]{1,0:T(8,128)(2,1)S(1)} %get-tuple-element.13.panel_ref, f32[8,512]{1,0:T(8,128)S(1)} %get-tuple-element.14.sums_ref, s16[2,4,8,72,128]{4,3,2,1,0:T(8,128)(2,1)S(1)} %bitcast.15), custom_call_target="tpu_custom_call" | custom-call | flops 2147483648 | bytes 10485760 | tf_op jit(solution)/shard_map/pallas_call | solution.py:383
  100.2 16.7 %all_to_all.48.received_ref = f32[8,72,128]{2,1,0:T(8,128)S(1)} all-to-all(f32[8,72,128]{2,1,0:T(8,128)S(1)} %shard_map.138), channel_id=1, replica_groups=mesh['zh'=8,'zl'=2,'x'=4,'narrow'=8] {'narrow'}, dimensions={0} | all-to-all | bytes 589824 | tf_op jit(solution)/shard_map/all_to_all | solution.py:407
  116.9 0.2 shard_map.139
  117.1 17.9 %all_to_all.49 = s16[8,72,128]{2,1,0:T(8,128)(2,1)S(1)} all-to-all(s16[8,72,128]{2,1,0:T(8,128)(2,1)S(1)} %shard_map.139), channel_id=1, replica_groups=mesh['zh'=8,'zl'=2,'x'=4,'narrow'=8] {'zh'}, dimensions={0} | all-to-all | bytes 294912 | tf_op jit(solution)/shard_map/all_to_all | solution.py:394
  135.0 25.5 %all-gather.2 = s16[64,72,128]{2,1,0:T(8,128)(2,1)S(1)} all-gather(s16[8,72,128]{2,1,0:T(8,128)(2,1)S(1)} %all_to_all.49), channel_id=2, replica_groups=mesh['zh'=8,'zl'=2,'x'=4,'narrow'=8] {'zl','x'}, dimensions={0}, use_global_device_ids=true | all-gather | bytes 1327104 | tf_op jit(solution)/shard_map/all_gather | solution.py:396
  160.4 4.2 %shard_map.140 = f32[8,72,128]{2,1,0:T(8,128)S(1)} custom-call(bf16[1024,4096]{1,0:T(8,128)(2,1)S(1)} %get-tuple-element.13.panel_ref, f32[8,512]{1,0:T(8,128)S(1)} %get-tuple-element.14.sums_ref, s16[2,4,8,72,128]{4,3,2,1,0:T(8,128)(2,1)S(1)} %bitcast.16), custom_call_target="tpu_custom_call" | custom-call | flops 2147483648 | bytes 10485760 | tf_op jit(solution)/shard_map/pallas_call | solution.py:383
  164.7 18.0 %all_to_all.50.received_ref = f32[8,72,128]{2,1,0:T(8,128)S(1)} all-to-all(f32[8,72,128]{2,1,0:T(8,128)S(1)} %shard_map.140), channel_id=1, replica_groups=mesh['zh'=8,'zl'=2,'x'=4,'narrow'=8] {'narrow'}, dimensions={0} | all-to-all | bytes 589824 | tf_op jit(solution)/shard_map/all_to_all | solution.py:407
  182.6 0.2 shard_map.141
  182.9 16.0 %all_to_all.51 = s16[8,72,128]{2,1,0:T(8,128)(2,1)S(1)} all-to-all(s16[8,72,128]{2,1,0:T(8,128)(2,1)S(1)} %shard_map.141), channel_id=1, replica_groups=mesh['zh'=8,'zl'=2,'x'=4,'narrow'=8] {'zh'}, dimensions={0} | all-to-all | bytes 294912 | tf_op jit(solution)/shard_map/all_to_all | solution.py:394
  198.9 0.2 broadcast_in_dim.24
  199.0 16.1 %all_to_all.52 = s16[8,8,72,128]{3,2,1,0:T(8,128)(2,1)S(1)} all-to-all(s16[8,8,72,128]{3,2,1,0:T(8,128)(2,1)S(1)} %broadcast_in_dim.24), channel_id=1, replica_groups=mesh['zh'=8,'zl'=2,'x'=4,'narrow'=8] {'zl','x'}, dimensions={0} | all-to-all | bytes 2359296 | tf_op jit(solution)/shard_map/all_to_all | solution.py:398
  215.1 0.0 copy-start.2
  215.1 0.0 copy-start.6
  215.1 4.2 %shard_map.142 = f32[8,72,128]{2,1,0:T(8,128)S(1)} custom-call(bf16[1024,4096]{1,0:T(8,128)(2,1)S(1)} %get-tuple-element.13.panel_ref, f32[8,512]{1,0:T(8,128)S(1)} %get-tuple-element.14.sums_ref, s16[2,4,8,72,128]{4,3,2,1,0:T(8,128)(2,1)S(1)} %bitcast.14), custom_call_target="tpu_custom_call" | custom-call | flops 2147483648 | bytes 10485760 | tf_op jit(solution)/shard_map/pallas_call | solution.py:383
  219.3 14.6 %all_to_all.53.received_ref = f32[8,72,128]{2,1,0:T(8,128)S(1)} all-to-all(f32[8,72,128]{2,1,0:T(8,128)S(1)} %shard_map.142), channel_id=1, replica_groups=mesh['zh'=8,'zl'=2,'x'=4,'narrow'=8] {'narrow'}, dimensions={0} | all-to-all | bytes 589824 | tf_op jit(solution)/shard_map/all_to_all | solution.py:407
  233.9 0.0 copy-done.2
  233.9 0.0 copy-done.6
  233.9 0.8 shard_map.143
Async XLA Ops:
  1.4 1.6 copy-start
  3.0 0.7 copy-start.1
  3.8 0.7 copy-start.5
  4.5 0.7 copy-start.8
  5.1 0.7 copy-start.9
  5.8 0.7 copy-start.10
  6.4 0.7 copy-start.11
  7.1 56.6 %copy-start.3 = (bf16[128,128]{1,0:T(8,128)(2,1)S(1)}, bf16[128,128]{1,0:T(8,128)(2,1)}, u32[]{:S(2)}) copy-start(bf16[128,128]{1,0:T(8,128)(2,1)} %w_self_ref.1) | copy-start | bytes 98308
  7.1 56.6 %copy-start.4 = (bf16[128,128]{1,0:T(8,128)(2,1)S(1)}, bf16[128,128]{1,0:T(8,128)(2,1)}, u32[]{:S(2)}) copy-start(bf16[128,128]{1,0:T(8,128)(2,1)} %w_neigh_ref.1) | copy-start | bytes 98308
  7.1 56.6 %copy-start.7 = (f32[128]{0:T(128)S(1)}, f32[128]{0:T(128)}, u32[]{:S(2)}) copy-start(f32[128]{0:T(128)} %param.20) | copy-start | bytes 1540
  215.1 18.9 %copy-start.2 = (bf16[128,256]{1,0:T(8,128)(2,1)S(1)}, bf16[128,256]{1,0:T(8,128)(2,1)}, u32[]{:S(2)}) copy-start(bf16[128,256]{1,0:T(8,128)(2,1)} %w_ref.1) | copy-start | bytes 196612
  215.1 18.9 %copy-start.6 = (f32[256]{0:T(256)S(1)}, f32[256]{0:T(256)}, u32[]{:S(2)}) copy-start(f32[256]{0:T(256)} %param.22) | copy-start | bytes 3076

commit v4 on v3

--- a/solution.py
+++ b/solution.py
@@ -98,6 +98,7 @@
     tiles_ref,
     linked_ref,
     dangling_ref,
+    turned_ref,
     index_ref,
     total,
     sems,
@@ -131,12 +132,18 @@
 
     features = features_ref[...]
     nodes = features.shape[0]
-    lists, capacity = send_ref.shape
+    capacity, lists = send_ref.shape
     per_row = 128 // capacity
     lane = lax.broadcasted_iota(i32, (1, 128), 1)
     row = lax.broadcasted_iota(i32, (nodes, 128), 0)
+    over = ((1,), (1,))
+    square = (lists, lists)
+    turn = lax.broadcasted_iota(i32, square, 0) == lax.broadcasted_iota(i32, square, 1)
+    turned_ref[...] = dot(
+        turn.astype(f32).astype(bf16), send_ref[...].astype(f32).astype(bf16), over
+    ).astype(i32)
     for m in range(per_row):
-        index_ref[:, pl.ds(m * capacity, capacity)] = send_ref[
+        index_ref[:, pl.ds(m * capacity, capacity)] = turned_ref[
             pl.ds(m, lists // per_row, stride=per_row), :
         ]
     for k in range(lists // per_row):
@@ -153,7 +160,6 @@
     eye = same.astype(f32).astype(bf16)
     linked = linked_ref[...]
     high = linked >> 6
-    over = ((1,), (1,))
     linked = 64.0 * dot(eye, high.astype(f32).astype(bf16), over) + dot(
         eye, (linked - (high << 6)).astype(f32).astype(bf16), over
     )
@@ -323,6 +329,7 @@
     node_total = row_total * wide
     degree = neighbors.shape[1]
 
+    keep = functools.partial(pltpu.with_memory_space_constraint, memory_space=pltpu.HBM)
     outgoing, panel, row_sums, own, far, marks = call(
         head_kernel,
         [
@@ -337,7 +344,7 @@
         in_specs=[pl.BlockSpec(memory_space=pltpu.HBM)] * 9,
         scratch=[
             pltpu.SMEM((1, wide), i32),
-            pltpu.VMEM((wide, capacity), i32),
+            pltpu.VMEM((capacity, wide), i32),
             pltpu.VMEM((nodes, width), bf16),
             pltpu.SMEM(tile_rows.shape[1:], i32),
             pltpu.SMEM(tile_rows.shape[1:], i32),
@@ -345,6 +352,7 @@
             pltpu.VMEM(tiles.shape[2:], bf16),
             pltpu.VMEM((degree, nodes), i32),
             pltpu.VMEM((1, nodes), i32),
+            pltpu.VMEM((wide, capacity), i32),
             pltpu.VMEM((wide * capacity // 128, 128), i32),
             pltpu.VMEM((row_total * col_total // (128 * 128), 128, 128), f32),
             pltpu.SemaphoreType.DMA((9,)),
@@ -353,15 +361,15 @@
         nbytes=20 << 20,
         limit=16 << 20,
     )(
-        send_count[0],
-        send_rows[0, 0],
-        features,
-        tile_rows[0],
-        tile_cols[0],
+        keep(send_count[0]),
+        keep(send_rows[0, 0].T),
+        keep(features),
+        keep(tile_rows[0]),
+        keep(tile_cols[0]),
         tile_count,
-        tiles[0, 0],
-        neighbors.T,
-        dangling[None, :],
+        keep(tiles[0, 0]),
+        keep(neighbors.T),
+        keep(dangling[None, :]),
     )
     received = lax.all_to_all(
         outgoing.reshape(wide, capacity, width),
@@ -392,16 +400,13 @@
 
     for repeat in range(ITERS):
         got = lax.all_to_all(packed, "zh", split_axis=0, concat_axis=0, tiled=True)
-        if repeat == 1:
-            got = lax.all_gather(got, ("zl", "x"), axis=0)
-        else:
-            got = lax.all_to_all(
-                jnp.broadcast_to(got[None], (zl * nx,) + got.shape),
-                ("zl", "x"),
-                split_axis=0,
-                concat_axis=0,
-                tiled=True,
-            )
+        got = lax.all_to_all(
+            jnp.broadcast_to(got[None], (zl * nx,) + got.shape),
+            ("zl", "x"),
+            split_axis=0,
+            concat_axis=0,
+            tiled=True,
+        )
         got = got.reshape((zl, nx) + got.shape[1:])
         partial = spread(got, repeat)
         sums = lax.all_to_all(partial, "narrow", split_axis=0, concat_axis=0, tiled=True)

time: 235 us -> 219 us (0.932)
  blocking collectives: 209 us -> 199 us
  local copies, waits for them, and re-layouts: 6.75 us -> 0.48 us
    all_gather x1 -> x0, blocking collectives: 25.5 us -> none  [body(): got = lax.all_gather(got, ('zl', 'x'), axis=0)]
    all_to_all x2 -> x3, blocking collectives: 31 us -> 47.5 us  [body(): lax.all_to_all(jnp.broadcast_to(got[None], (zl * nx,) + got.shape), ('zl'...]
    unnamed x25 -> x12, local copies, waits for them, and re-layouts: 6.44 us -> 0.02 us
    all_to_all x3, blocking collectives: 52.2 us -> 56.4 us  [body(): got = lax.all_to_all(packed, 'zh', split_axis=0, concat_axis=0, tiled=True)]
    all_to_all x3, blocking collectives: 49.3 us -> 46.6 us  [body(): lax.all_to_all(partial, 'narrow', split_axis=0, concat_axis=0, tiled=True)]
where the time goes in v4:
time: 219 us
  blocking collectives  199 us (91%)
  Pallas kernels  18.6 us (8%)
    all_to_all x3, blocking collectives, body(): got = lax.all_to_all(packed, 'zh', split_axis=0, concat_axis=0, tiled=True)  56.4 us
    all_to_all x1, blocking collectives, body(): lax.all_to_all(outgoing.reshape(wide, capacity, width), ('zh', 'zl', 'x')...  48.4 us
    all_to_all x3, blocking collectives, body(): lax.all_to_all(jnp.broadcast_to(got[None], (zl * nx,) + got.shape), ('zl'...  47.5 us
    all_to_all x3, blocking collectives, body(): lax.all_to_all(partial, 'narrow', split_axis=0, concat_axis=0, tiled=True)  46.6 us
    pallas_call x3, Pallas kernels, spread(): call(functools.partial(spread_kernel, node_total, (zh, zl, nx), repeat ==...  11.1 us
    pallas_call x1, Pallas kernels, body(): call(head_kernel, [shape((slots, width), bf16), shape((2 * row_total, col...  5.85 us

profile of v4, /device:TPU:1, one launch (start us, length us, event | category | flops | bytes accessed | tf_op | source)
XLA Modules:
  0.0 218.7 jit_solution(1120531217412444450)
XLA Ops:
  0.7 0.0 copy-start
  0.7 0.0 copy-start.2
  0.7 0.0 copy-start.3
  0.7 0.0 copy-start.5
  0.7 5.9 %shard_map.136 = (bf16[2048,128]{1,0:T(8,128)(2,1)S(1)}, bf16[1024,4096]{1,0:T(8,128)(2,1)S(1)}, f32[8,512]{1,0:T(8,128)S(1)}, bf16[64,64]{1,0:T(8,128)(2,1)S(1)...) custom-call(s32[1,64]{1,0:T(1,128)} %bitcast.26, s32[32,64]{1,0:T(8,128)} %bitcast.24, ...), custom_call_target="tpu_custom_call" | custom-call | flops 16777216 | bytes 20971520 | tf_op jit(solution)/shard_map/pallas_call | solution.py:333
  6.6 48.4 %all_to_all.50 = bf16[64,32,128]{2,1,0:T(8,128)(2,1)S(1)} all-to-all(bf16[64,32,128]{2,1,0:T(8,128)(2,1)S(1)} %bitcast.20), channel_id=1, replica_groups=mesh['zh'=8,'zl'=2,'x'=4,'narrow'=8] {'zh','zl','x'}, dimensions={0} | all-to-all | bytes 1048576 | tf_op jit(solution)/shard_map/all_to_all | solution.py:374
  55.0 0.0 copy-done
  55.0 0.0 copy-done.2
  55.0 0.0 copy-done.3
  55.0 0.0 copy-done.5
  55.0 0.4 shard_map.137
  55.4 19.0 %all_to_all.51 = s16[8,72,128]{2,1,0:T(8,128)(2,1)S(1)} all-to-all(s16[8,72,128]{2,1,0:T(8,128)(2,1)S(1)} %get-tuple-element.19), channel_id=1, replica_groups=mesh['zh'=8,'zl'=2,'x'=4,'narrow'=8] {'zh'}, dimensions={0} | all-to-all | bytes 294912 | tf_op jit(solution)/shard_map/all_to_all | solution.py:402
  74.4 0.2 broadcast_in_dim.14
  74.6 15.5 %all_to_all.52 = s16[8,8,72,128]{3,2,1,0:T(8,128)(2,1)S(1)} all-to-all(s16[8,8,72,128]{3,2,1,0:T(8,128)(2,1)S(1)} %broadcast_in_dim.14), channel_id=1, replica_groups=mesh['zh'=8,'zl'=2,'x'=4,'narrow'=8] {'zl','x'}, dimensions={0} | all-to-all | bytes 2359296 | tf_op jit(solution)/shard_map/all_to_all | solution.py:403
  90.1 2.6 %shard_map.138 = f32[8,72,128]{2,1,0:T(8,128)S(1)} custom-call(bf16[1024,4096]{1,0:T(8,128)(2,1)S(1)} %get-tuple-element.13.panel_ref, f32[8,512]{1,0:T(8,128)S(1)} %get-tuple-element.14.sums_ref, s16[2,4,8,72,128]{4,3,2,1,0:T(8,128)(2,1)S(1)} %bitcast.17), custom_call_target="tpu_custom_call" | custom-call | flops 2147483648 | bytes 10485760 | tf_op jit(solution)/shard_map/pallas_call | solution.py:391
  92.7 18.3 %all_to_all.53.received_ref = f32[8,72,128]{2,1,0:T(8,128)S(1)} all-to-all(f32[8,72,128]{2,1,0:T(8,128)S(1)} %shard_map.138), channel_id=1, replica_groups=mesh['zh'=8,'zl'=2,'x'=4,'narrow'=8] {'narrow'}, dimensions={0} | all-to-all | bytes 589824 | tf_op jit(solution)/shard_map/all_to_all | solution.py:412
  111.0 0.2 shard_map.139
  111.3 18.3 %all_to_all.54 = s16[8,72,128]{2,1,0:T(8,128)(2,1)S(1)} all-to-all(s16[8,72,128]{2,1,0:T(8,128)(2,1)S(1)} %shard_map.139), channel_id=1, replica_groups=mesh['zh'=8,'zl'=2,'x'=4,'narrow'=8] {'zh'}, dimensions={0} | all-to-all | bytes 294912 | tf_op jit(solution)/shard_map/all_to_all | solution.py:402
  129.6 0.2 broadcast_in_dim.30
  129.7 16.0 %all_to_all.55 = s16[8,8,72,128]{3,2,1,0:T(8,128)(2,1)S(1)} all-to-all(s16[8,8,72,128]{3,2,1,0:T(8,128)(2,1)S(1)} %broadcast_in_dim.30), channel_id=1, replica_groups=mesh['zh'=8,'zl'=2,'x'=4,'narrow'=8] {'zl','x'}, dimensions={0} | all-to-all | bytes 2359296 | tf_op jit(solution)/shard_map/all_to_all | solution.py:403
  145.7 4.2 %shard_map.140 = f32[8,72,128]{2,1,0:T(8,128)S(1)} custom-call(bf16[1024,4096]{1,0:T(8,128)(2,1)S(1)} %get-tuple-element.13.panel_ref, f32[8,512]{1,0:T(8,128)S(1)} %get-tuple-element.14.sums_ref, s16[2,4,8,72,128]{4,3,2,1,0:T(8,128)(2,1)S(1)} %bitcast.18), custom_call_target="tpu_custom_call" | custom-call | flops 2147483648 | bytes 10485760 | tf_op jit(solution)/shard_map/pallas_call | solution.py:391
  149.9 14.2 %all_to_all.56.received_ref = f32[8,72,128]{2,1,0:T(8,128)S(1)} all-to-all(f32[8,72,128]{2,1,0:T(8,128)S(1)} %shard_map.140), channel_id=1, replica_groups=mesh['zh'=8,'zl'=2,'x'=4,'narrow'=8] {'narrow'}, dimensions={0} | all-to-all | bytes 589824 | tf_op jit(solution)/shard_map/all_to_all | solution.py:412
  164.1 0.2 shard_map.141
  164.3 19.1 %all_to_all.57 = s16[8,72,128]{2,1,0:T(8,128)(2,1)S(1)} all-to-all(s16[8,72,128]{2,1,0:T(8,128)(2,1)S(1)} %shard_map.141), channel_id=1, replica_groups=mesh['zh'=8,'zl'=2,'x'=4,'narrow'=8] {'zh'}, dimensions={0} | all-to-all | bytes 294912 | tf_op jit(solution)/shard_map/all_to_all | solution.py:402
  183.4 0.2 broadcast_in_dim.31
  183.5 16.0 %all_to_all.58 = s16[8,8,72,128]{3,2,1,0:T(8,128)(2,1)S(1)} all-to-all(s16[8,8,72,128]{3,2,1,0:T(8,128)(2,1)S(1)} %broadcast_in_dim.31), channel_id=1, replica_groups=mesh['zh'=8,'zl'=2,'x'=4,'narrow'=8] {'zl','x'}, dimensions={0} | all-to-all | bytes 2359296 | tf_op jit(solution)/shard_map/all_to_all | solution.py:403
  199.5 0.0 copy-start.1
  199.5 0.0 copy-start.4
  199.5 4.2 %shard_map.142 = f32[8,72,128]{2,1,0:T(8,128)S(1)} custom-call(bf16[1024,4096]{1,0:T(8,128)(2,1)S(1)} %get-tuple-element.13.panel_ref, f32[8,512]{1,0:T(8,128)S(1)} %get-tuple-element.14.sums_ref, s16[2,4,8,72,128]{4,3,2,1,0:T(8,128)(2,1)S(1)} %bitcast.16), custom_call_target="tpu_custom_call" | custom-call | flops 2147483648 | bytes 10485760 | tf_op jit(solution)/shard_map/pallas_call | solution.py:391
  203.7 14.2 %all_to_all.59.received_ref = f32[8,72,128]{2,1,0:T(8,128)S(1)} all-to-all(f32[8,72,128]{2,1,0:T(8,128)S(1)} %shard_map.142), channel_id=1, replica_groups=mesh['zh'=8,'zl'=2,'x'=4,'narrow'=8] {'narrow'}, dimensions={0} | all-to-all | bytes 589824 | tf_op jit(solution)/shard_map/all_to_all | solution.py:412
  217.9 0.0 copy-done.1
  217.9 0.0 copy-done.4
  217.9 0.8 shard_map.143
Async XLA Ops:
  0.7 54.3 %copy-start = (bf16[64,128]{1,0:T(8,128)(2,1)S(1)}, bf16[64,128]{1,0:T(8,128)(2,1)}, u32[]{:S(2)}) copy-start(bf16[64,128]{1,0:T(8,128)(2,1)} %features_ref.1) | copy-start | bytes 49156
  0.7 54.3 %copy-start.2 = (bf16[128,128]{1,0:T(8,128)(2,1)S(1)}, bf16[128,128]{1,0:T(8,128)(2,1)}, u32[]{:S(2)}) copy-start(bf16[128,128]{1,0:T(8,128)(2,1)} %w_self_ref.1) | copy-start | bytes 98308
  0.7 54.3 %copy-start.3 = (bf16[128,128]{1,0:T(8,128)(2,1)S(1)}, bf16[128,128]{1,0:T(8,128)(2,1)}, u32[]{:S(2)}) copy-start(bf16[128,128]{1,0:T(8,128)(2,1)} %w_neigh_ref.1) | copy-start | bytes 98308
  0.7 54.3 %copy-start.5 = (f32[128]{0:T(128)S(1)}, f32[128]{0:T(128)}, u32[]{:S(2)}) copy-start(f32[128]{0:T(128)} %param.20) | copy-start | bytes 1540
  199.5 18.4 %copy-start.1 = (bf16[128,256]{1,0:T(8,128)(2,1)S(1)}, bf16[128,256]{1,0:T(8,128)(2,1)}, u32[]{:S(2)}) copy-start(bf16[128,256]{1,0:T(8,128)(2,1)} %w_ref.1) | copy-start | bytes 196612
  199.5 18.4 %copy-start.4 = (f32[256]{0:T(256)S(1)}, f32[256]{0:T(256)}, u32[]{:S(2)}) copy-start(f32[256]{0:T(256)} %param.22) | copy-start | bytes 3076

commit v5 on v4

--- a/solution.py
+++ b/solution.py
@@ -85,6 +85,7 @@
     dangling_hbm,
     outgoing_ref,
     panel_ref,
+    total,
     sums_ref,
     own_ref,
     far_ref,
@@ -100,7 +101,7 @@
     dangling_ref,
     turned_ref,
     index_ref,
-    total,
+    whole_ref,
     sems,
 ):
     pairs = (
@@ -192,18 +193,22 @@
 
     lax.fori_loop(0, used_ref[0, 0], place, 0)
 
-    def store(r, _):
-        at = pl.ds(pl.multiple_of(r * 128, 128), 128)
-        below = pl.ds(pl.multiple_of((r + row_tiles) * 128, 128), 128)
-        whole = jnp.zeros((128, 128), f32)
+    def store(g, _):
+        at = pl.ds(pl.multiple_of(g * 16, 16), 16)
+        below = pl.ds(pl.multiple_of(g * 16 + row_tiles * 128, 16), 16)
+        r = g // 8
+        inner = pl.ds(pl.multiple_of((g % 8) * 16, 16), 16)
+        whole = jnp.zeros((16, 128), f32)
         for c in range(col_tiles):
-            tile = total[r * col_tiles + c]
+            tile = total[r * col_tiles + c, inner, :]
             whole = whole + tile
             panel_ref[at, pl.ds(c * 128, 128)], panel_ref[below, pl.ds(c * 128, 128)] = split(tile)
-        sums_ref[:, at] = lane_sums(whole)
+        whole_ref[at, :] = whole
         return 0
 
-    lax.fori_loop(0, row_tiles, store, 0)
+    lax.fori_loop(0, row_tiles * 8, store, 0)
+    for r in range(row_tiles):
+        sums_ref[:, pl.ds(r * 128, 128)] = lane_sums(whole_ref[pl.ds(r * 128, 128), :])
 
 
 def hidden_kernel(
@@ -228,7 +233,9 @@
     encode(hidden, jnp.ones((1, hidden.shape[1]), f32), dangling_ref[...], out_ref)
 
 
-def spread_kernel(node_total, parts, first, panel_ref, sums_ref, packed_ref, out_ref, z_parts, s_row):
+def spread_kernel(
+    node_total, parts, first, panel_ref, sums_ref, packed_ref, out_ref, z_parts, s_row
+):
     zh, zl, nx = parts
     half = panel_ref.shape[0] // 2
     nodes = 64
@@ -258,12 +265,14 @@
     if first:
         s_sum = sums_ref[...]
     else:
-        part = jnp.zeros((half, 128), f32)
-        for c in range(panel_ref.shape[1] // 128):
-            at = pl.ds(c * 128, 128)
-            tile = panel_ref[:half, at].astype(f32) + panel_ref[half:, at].astype(f32)
-            part = part + tile * s_row[0:1, at]
-        s_sum = lane_sums(part)
+        col_tiles = panel_ref.shape[1] // 128
+        pieces = []
+        for r in range(half // 128):
+            part = sums_ref[r * col_tiles] * s_row[0:1, pl.ds(0, 128)]
+            for c in range(1, col_tiles):
+                part = part + sums_ref[r * col_tiles + c] * s_row[0:1, pl.ds(c * 128, 128)]
+            pieces.append(lane_sums(part))
+        s_sum = jnp.concatenate(pieces, axis=1)
     for b in range(half // nodes):
         out_ref[b, pl.ds(0, nodes), :] = z_sum[b * nodes : (b + 1) * nodes]
         two = s_sum[:, (b // 2) * 128 : (b // 2) * 128 + 128]
@@ -330,11 +339,12 @@
     degree = neighbors.shape[1]
 
     keep = functools.partial(pltpu.with_memory_space_constraint, memory_space=pltpu.HBM)
-    outgoing, panel, row_sums, own, far, marks = call(
+    outgoing, panel, total, row_sums, own, far, marks = call(
         head_kernel,
         [
             shape((slots, width), bf16),
             shape((2 * row_total, col_total), bf16),
+            shape((row_total * col_total // (128 * 128), 128, 128), f32),
             shape((8, row_total), f32),
             shape((nodes, nodes), bf16),
             shape((nodes, slots), bf16),
@@ -354,7 +364,7 @@
             pltpu.VMEM((1, nodes), i32),
             pltpu.VMEM((wide, capacity), i32),
             pltpu.VMEM((wide * capacity // 128, 128), i32),
-            pltpu.VMEM((row_total * col_total // (128 * 128), 128, 128), f32),
+            pltpu.VMEM((row_total, 128), f32),
             pltpu.SemaphoreType.DMA((9,)),
         ],
         flops=1 << 24,
@@ -396,7 +406,7 @@
             flops=2 * 2 * row_total * col_total * 256,
             nbytes=10 << 20,
             limit=12 << 20,
-        )(panel, row_sums, packed)
+        )(panel, row_sums if repeat == 0 else total, packed)
 
     for repeat in range(ITERS):
         got = lax.all_to_all(packed, "zh", split_axis=0, concat_axis=0, tiled=True)

time: 219 us -> 217 us (level)
  no operation moved by 1% of the time
where the time goes in v5:
time: 217 us
  blocking collectives  199 us (92%)
  Pallas kernels  16.6 us (8%)
    all_to_all x3, blocking collectives, body(): got = lax.all_to_all(packed, 'zh', split_axis=0, concat_axis=0, tiled=True)  55.8 us
    all_to_all x1, blocking collectives, body(): lax.all_to_all(outgoing.reshape(wide, capacity, width), ('zh', 'zl', 'x')...  49.4 us
    all_to_all x3, blocking collectives, body(): lax.all_to_all(jnp.broadcast_to(got[None], (zl * nx,) + got.shape), ('zl'...  47.5 us
    all_to_all x3, blocking collectives, body(): lax.all_to_all(partial, 'narrow', split_axis=0, concat_axis=0, tiled=True)  46.2 us
    pallas_call x3, Pallas kernels, spread(): call(functools.partial(spread_kernel, node_total, (zh, zl, nx), repeat ==...  9.85 us
    pallas_call x1, Pallas kernels, body(): call(head_kernel, [shape((slots, width), bf16), shape((2 * row_total, col...  5.11 us

profile of v5, /device:TPU:1, one launch (start us, length us, event | category | flops | bytes accessed | tf_op | source)
XLA Modules:
  0.0 216.8 jit_solution(1715966184954941600)
XLA Ops:
  0.7 0.0 copy-start
  0.7 0.0 copy-start.2
  0.7 0.0 copy-start.3
  0.7 0.0 copy-start.5
  0.7 5.1 %shard_map.136 = (bf16[2048,128]{1,0:T(8,128)(2,1)S(1)}, bf16[1024,4096]{1,0:T(8,128)(2,1)S(1)}, f32[128,128,128]{2,1,0:T(8,128)S(1)}, f32[8,512]{1,0:T(8,128)S(...) custom-call(s32[1,64]{1,0:T(1,128)} %bitcast.26, s32[32,64]{1,0:T(8,128)} %bitcast.24, ...), custom_call_target="tpu_custom_call" | custom-call | flops 16777216 | bytes 20971520 | tf_op jit(solution)/shard_map/pallas_call | solution.py:342
  5.8 49.4 %all_to_all.50 = bf16[64,32,128]{2,1,0:T(8,128)(2,1)S(1)} all-to-all(bf16[64,32,128]{2,1,0:T(8,128)(2,1)S(1)} %bitcast.20), channel_id=1, replica_groups=mesh['zh'=8,'zl'=2,'x'=4,'narrow'=8] {'zh','zl','x'}, dimensions={0} | all-to-all | bytes 1048576 | tf_op jit(solution)/shard_map/all_to_all | solution.py:384
  55.2 0.0 copy-done
  55.2 0.0 copy-done.2
  55.2 0.0 copy-done.3
  55.3 0.0 copy-done.5
  55.3 0.4 shard_map.137
  55.7 18.4 %all_to_all.51 = s16[8,72,128]{2,1,0:T(8,128)(2,1)S(1)} all-to-all(s16[8,72,128]{2,1,0:T(8,128)(2,1)S(1)} %get-tuple-element.21), channel_id=1, replica_groups=mesh['zh'=8,'zl'=2,'x'=4,'narrow'=8] {'zh'}, dimensions={0} | all-to-all | bytes 294912 | tf_op jit(solution)/shard_map/all_to_all | solution.py:412
  74.1 0.2 broadcast_in_dim.14
  74.2 15.4 %all_to_all.52 = s16[8,8,72,128]{3,2,1,0:T(8,128)(2,1)S(1)} all-to-all(s16[8,8,72,128]{3,2,1,0:T(8,128)(2,1)S(1)} %broadcast_in_dim.14), channel_id=1, replica_groups=mesh['zh'=8,'zl'=2,'x'=4,'narrow'=8] {'zl','x'}, dimensions={0} | all-to-all | bytes 2359296 | tf_op jit(solution)/shard_map/all_to_all | solution.py:413
  89.7 2.7 %shard_map.138 = f32[8,72,128]{2,1,0:T(8,128)S(1)} custom-call(bf16[1024,4096]{1,0:T(8,128)(2,1)S(1)} %get-tuple-element.14.panel_ref, f32[8,512]{1,0:T(8,128)S(1)} %get-tuple-element.16.sums_ref, s16[2,4,8,72,128]{4,3,2,1,0:T(8,128)(2,1)S(1)} %bitcast.17), custom_call_target="tpu_custom_call" | custom-call | flops 2147483648 | bytes 10485760 | tf_op jit(solution)/shard_map/pallas_call | solution.py:401
  92.3 17.9 %all_to_all.53.received_ref = f32[8,72,128]{2,1,0:T(8,128)S(1)} all-to-all(f32[8,72,128]{2,1,0:T(8,128)S(1)} %shard_map.138), channel_id=1, replica_groups=mesh['zh'=8,'zl'=2,'x'=4,'narrow'=8] {'narrow'}, dimensions={0} | all-to-all | bytes 589824 | tf_op jit(solution)/shard_map/all_to_all | solution.py:422
  110.2 0.2 shard_map.139
  110.5 18.5 %all_to_all.54 = s16[8,72,128]{2,1,0:T(8,128)(2,1)S(1)} all-to-all(s16[8,72,128]{2,1,0:T(8,128)(2,1)S(1)} %shard_map.139), channel_id=1, replica_groups=mesh['zh'=8,'zl'=2,'x'=4,'narrow'=8] {'zh'}, dimensions={0} | all-to-all | bytes 294912 | tf_op jit(solution)/shard_map/all_to_all | solution.py:412
  128.9 0.2 broadcast_in_dim.30
  129.1 16.0 %all_to_all.55 = s16[8,8,72,128]{3,2,1,0:T(8,128)(2,1)S(1)} all-to-all(s16[8,8,72,128]{3,2,1,0:T(8,128)(2,1)S(1)} %broadcast_in_dim.30), channel_id=1, replica_groups=mesh['zh'=8,'zl'=2,'x'=4,'narrow'=8] {'zl','x'}, dimensions={0} | all-to-all | bytes 2359296 | tf_op jit(solution)/shard_map/all_to_all | solution.py:413
  145.1 3.6 %shard_map.140 = f32[8,72,128]{2,1,0:T(8,128)S(1)} custom-call(bf16[1024,4096]{1,0:T(8,128)(2,1)S(1)} %get-tuple-element.14.panel_ref, f32[128,128,128]{2,1,0:T(8,128)S(1)} %get-tuple-element.15.sums_ref, s16[2,4,8,72,128]{4,3,2,1,0:T(8,128)(2,1)S(1)} %bitcast.18), custom_call_target="tpu_custom_call" | custom-call | flops 2147483648 | bytes 10485760 | tf_op jit(solution)/shard_map/pallas_call | solution.py:401
  148.7 14.1 %all_to_all.56.received_ref = f32[8,72,128]{2,1,0:T(8,128)S(1)} all-to-all(f32[8,72,128]{2,1,0:T(8,128)S(1)} %shard_map.140), channel_id=1, replica_groups=mesh['zh'=8,'zl'=2,'x'=4,'narrow'=8] {'narrow'}, dimensions={0} | all-to-all | bytes 589824 | tf_op jit(solution)/shard_map/all_to_all | solution.py:422
  162.9 0.2 shard_map.141
  163.1 19.0 %all_to_all.57 = s16[8,72,128]{2,1,0:T(8,128)(2,1)S(1)} all-to-all(s16[8,72,128]{2,1,0:T(8,128)(2,1)S(1)} %shard_map.141), channel_id=1, replica_groups=mesh['zh'=8,'zl'=2,'x'=4,'narrow'=8] {'zh'}, dimensions={0} | all-to-all | bytes 294912 | tf_op jit(solution)/shard_map/all_to_all | solution.py:412
  182.0 0.2 broadcast_in_dim.31
  182.2 16.0 %all_to_all.58 = s16[8,8,72,128]{3,2,1,0:T(8,128)(2,1)S(1)} all-to-all(s16[8,8,72,128]{3,2,1,0:T(8,128)(2,1)S(1)} %broadcast_in_dim.31), channel_id=1, replica_groups=mesh['zh'=8,'zl'=2,'x'=4,'narrow'=8] {'zl','x'}, dimensions={0} | all-to-all | bytes 2359296 | tf_op jit(solution)/shard_map/all_to_all | solution.py:413
  198.2 0.0 copy-start.1
  198.2 0.0 copy-start.4
  198.2 3.6 %shard_map.142 = f32[8,72,128]{2,1,0:T(8,128)S(1)} custom-call(bf16[1024,4096]{1,0:T(8,128)(2,1)S(1)} %get-tuple-element.14.panel_ref, f32[128,128,128]{2,1,0:T(8,128)S(1)} %get-tuple-element.15.sums_ref, s16[2,4,8,72,128]{4,3,2,1,0:T(8,128)(2,1)S(1)} %bitcast.16), custom_call_target="tpu_custom_call" | custom-call | flops 2147483648 | bytes 10485760 | tf_op jit(solution)/shard_map/pallas_call | solution.py:401
  201.8 14.1 %all_to_all.59.received_ref = f32[8,72,128]{2,1,0:T(8,128)S(1)} all-to-all(f32[8,72,128]{2,1,0:T(8,128)S(1)} %shard_map.142), channel_id=1, replica_groups=mesh['zh'=8,'zl'=2,'x'=4,'narrow'=8] {'narrow'}, dimensions={0} | all-to-all | bytes 589824 | tf_op jit(solution)/shard_map/all_to_all | solution.py:422
  216.0 0.0 copy-done.1
  216.0 0.0 copy-done.4
  216.0 0.8 shard_map.143
Async XLA Ops:
  0.7 54.6 %copy-start = (bf16[64,128]{1,0:T(8,128)(2,1)S(1)}, bf16[64,128]{1,0:T(8,128)(2,1)}, u32[]{:S(2)}) copy-start(bf16[64,128]{1,0:T(8,128)(2,1)} %features_ref.1) | copy-start | bytes 49156
  0.7 54.6 %copy-start.2 = (bf16[128,128]{1,0:T(8,128)(2,1)S(1)}, bf16[128,128]{1,0:T(8,128)(2,1)}, u32[]{:S(2)}) copy-start(bf16[128,128]{1,0:T(8,128)(2,1)} %w_self_ref.1) | copy-start | bytes 98308
  0.7 54.6 %copy-start.3 = (bf16[128,128]{1,0:T(8,128)(2,1)S(1)}, bf16[128,128]{1,0:T(8,128)(2,1)}, u32[]{:S(2)}) copy-start(bf16[128,128]{1,0:T(8,128)(2,1)} %w_neigh_ref.1) | copy-start | bytes 98308
  0.7 54.6 %copy-start.5 = (f32[128]{0:T(128)S(1)}, f32[128]{0:T(128)}, u32[]{:S(2)}) copy-start(f32[128]{0:T(128)} %param.20) | copy-start | bytes 1540
  198.2 17.7 %copy-start.1 = (bf16[128,256]{1,0:T(8,128)(2,1)S(1)}, bf16[128,256]{1,0:T(8,128)(2,1)}, u32[]{:S(2)}) copy-start(bf16[128,256]{1,0:T(8,128)(2,1)} %w_ref.1) | copy-start | bytes 196612
  198.2 17.7 %copy-start.4 = (f32[256]{0:T(256)S(1)}, f32[256]{0:T(256)}, u32[]{:S(2)}) copy-start(f32[256]{0:T(256)} %param.22) | copy-start | bytes 3076

commit v6 on v5

--- a/solution.py
+++ b/solution.py
@@ -236,16 +236,14 @@
 def spread_kernel(
     node_total, parts, first, panel_ref, sums_ref, packed_ref, out_ref, z_parts, s_row
 ):
-    zh, zl, nx = parts
     half = panel_ref.shape[0] // 2
     nodes = 64
     d_all = jnp.zeros((1, 128), f32)
     ds_all = jnp.zeros((1, 128), f32)
     lane = lax.broadcasted_iota(i32, (1, 128), 1)
     before = None
-    for a in range(zh * zl * nx):
-        h, m, x = a // (zl * nx), (a // nx) % zl, a % nx
-        codes = packed_ref[m, x, h].astype(i32).astype(f32)
+    for a, (i, j) in enumerate(parts):
+        codes = packed_ref[i, j].astype(i32).astype(f32)
         tail = codes[nodes:]
         step = jnp.exp2(tail * (1.0 / 256.0)) * (1.0 / TOP)
         hi, lo = split(codes[:nodes] * step[0:1])
@@ -328,8 +326,8 @@
 ):
     shape = jax.ShapeDtypeStruct
     nodes, width = features.shape
-    zh, zl, nx = (lax.axis_size(name) for name in ("zh", "zl", "x"))
-    wide = zh * zl * nx
+    sizes = {name: lax.axis_size(name) for name in ("zh", "zl", "xh", "xl")}
+    wide = sizes["zh"] * sizes["zl"] * sizes["xh"] * sizes["xl"]
     narrow = lax.axis_size("narrow")
     capacity = send_rows.shape[-1]
     slots = wide * capacity
@@ -383,13 +381,13 @@
     )
     received = lax.all_to_all(
         outgoing.reshape(wide, capacity, width),
-        ("zh", "zl", "x"),
+        ("zh", "zl", "xh", "xl"),
         split_axis=0,
         concat_axis=0,
         tiled=True,
     ).reshape(slots, width)
 
-    packed_shape = shape((zh, nodes + 8, width), i16)
+    packed_shape = shape((sizes["zh"] * 2, nodes + 8, width), i16)
     hidden, packed = call(
         functools.partial(hidden_kernel, degree),
         [shape((nodes, width), f32), packed_shape],
@@ -397,9 +395,9 @@
         limit=8 << 20,
     )(features, received, own, far, w_self, w_neigh, bias_hidden[None, :], marks)
 
-    def spread(packed, repeat):
+    def spread(packed, repeat, parts):
         return call(
-            functools.partial(spread_kernel, node_total, (zh, zl, nx), repeat == 0),
+            functools.partial(spread_kernel, node_total, parts, repeat == 0),
             shape((narrow, nodes + 8, width), f32),
             3,
             scratch=[pltpu.VMEM((col_total, 2 * width), bf16), pltpu.VMEM((8, col_total), f32)],
@@ -408,17 +406,36 @@
             limit=12 << 20,
         )(panel, row_sums if repeat == 0 else total, packed)
 
+    def places(one, two):
+        found = []
+        for a in range(wide):
+            at, rest = {}, a
+            for name in ("xl", "xh", "zl", "zh"):
+                at[name], rest = rest % sizes[name], rest // sizes[name]
+            found.append(
+                tuple(
+                    functools.reduce(lambda n, name: n * sizes[name] + at[name], names, 0)
+                    for names in (two, one)
+                )
+            )
+        return tuple(found)
+
+    routes = ((("zh", "zl"), ("xh", "xl")), (("zh", "zl"), ("xh", "xl")), (("zh", "xh"), ("zl", "xl")))
     for repeat in range(ITERS):
-        got = lax.all_to_all(packed, "zh", split_axis=0, concat_axis=0, tiled=True)
-        got = lax.all_to_all(
-            jnp.broadcast_to(got[None], (zl * nx,) + got.shape),
-            ("zl", "x"),
-            split_axis=0,
-            concat_axis=0,
-            tiled=True,
-        )
-        got = got.reshape((zl, nx) + got.shape[1:])
-        partial = spread(got, repeat)
+        one, two = routes[repeat]
+        got = lax.all_to_all(packed, one, split_axis=0, concat_axis=0, tiled=True)
+        if repeat == 1:
+            got = lax.all_gather(got, two, axis=0)
+        else:
+            copies = sizes[two[0]] * sizes[two[1]]
+            got = lax.all_to_all(
+                jnp.broadcast_to(got[None], (copies,) + got.shape),
+                two,
+                split_axis=0,
+                concat_axis=0,
+                tiled=True,
+            )
+        partial = spread(got, repeat, places(one, two))
         sums = lax.all_to_all(partial, "narrow", split_axis=0, concat_axis=0, tiled=True)
         if repeat < ITERS - 1:
             packed = call(step_kernel, packed_shape, 3, limit=4 << 20)(sums, hidden, marks)
@@ -429,12 +446,8 @@
 
 def solution(mesh):
     wide, narrow = mesh.devices.shape
-    nx = 4 if wide % 64 == 0 else 2
-    zl = 2
-    split_mesh = Mesh(
-        mesh.devices.reshape(wide // (zl * nx), zl, nx, narrow), ("zh", "zl", "x", "narrow")
-    )
-    wide_axes = ("zh", "zl", "x")
+    wide_axes = ("zh", "zl", "xh", "xl")
+    split_mesh = Mesh(mesh.devices.reshape(wide // 8, 2, 2, 2, narrow), wide_axes + ("narrow",))
     all_axes = wide_axes + ("narrow",)
     in_specs = (
         P(all_axes, None),

time: 217 us -> 232 us (1.069)
  blocking collectives: 199 us -> 214 us
    all_gather x0 -> x1, blocking collectives: none -> 12.5 us  [body(): got = lax.all_gather(got, two, axis=0)]
    all_to_all x3, blocking collectives: 46.2 us -> 51.4 us  [body(): lax.all_to_all(partial, 'narrow', split_axis=0, concat_axis=0, tiled=True)]
    all_to_all x7 -> x6, blocking collectives: 153 us -> 150 us  [the longest x3 69.5 us: body(): got = lax.all_to_all(packed, one, split_axis=0, concat_axis=0, tiled=True)]
where the time goes in v6:
time: 232 us
  blocking collectives  214 us (92%)
  Pallas kernels  16.6 us (7%)
    all_to_all x3, blocking collectives, body(): got = lax.all_to_all(packed, one, split_axis=0, concat_axis=0, tiled=True)  69.5 us
    all_to_all x3, blocking collectives, body(): lax.all_to_all(partial, 'narrow', split_axis=0, concat_axis=0, tiled=True)  51.4 us
    all_to_all x1, blocking collectives, body(): lax.all_to_all(outgoing.reshape(wide, capacity, width), ('zh', 'zl', 'xh'...  49.4 us
    all_to_all x2, blocking collectives, body(): lax.all_to_all(jnp.broadcast_to(got[None], (copies,) + got.shape), two, s...  31.5 us
    all_gather x1, blocking collectives, body(): got = lax.all_gather(got, two, axis=0)  12.5 us
    pallas_call x3, Pallas kernels, spread(): call(functools.partial(spread_kernel, node_total, parts, repeat == 0), sh...  9.84 us
    pallas_call x1, Pallas kernels, body(): call(head_kernel, [shape((slots, width), bf16), shape((2 * row_total, col...  5.11 us

profile of v6, /device:TPU:1, one launch (start us, length us, event | category | flops | bytes accessed | tf_op | source)
XLA Modules:
  0.0 232.0 jit_solution(8467386856527898029)
XLA Ops:
  0.7 0.0 copy-start
  0.7 0.0 copy-start.2
  0.7 0.0 copy-start.3
  0.7 0.0 copy-start.5
  0.7 5.1 %shard_map.136 = (bf16[2048,128]{1,0:T(8,128)(2,1)S(1)}, bf16[1024,4096]{1,0:T(8,128)(2,1)S(1)}, f32[128,128,128]{2,1,0:T(8,128)S(1)}, f32[8,512]{1,0:T(8,128)S(...) custom-call(s32[1,64]{1,0:T(1,128)} %bitcast.22, s32[32,64]{1,0:T(8,128)} %bitcast.20, ...), custom_call_target="tpu_custom_call" | custom-call | flops 16777216 | bytes 20971520 | tf_op jit(solution)/shard_map/pallas_call | solution.py:340
  5.8 49.4 %all_to_all.45 = bf16[64,32,128]{2,1,0:T(8,128)(2,1)S(1)} all-to-all(bf16[64,32,128]{2,1,0:T(8,128)(2,1)S(1)} %bitcast.16), channel_id=1, replica_groups=mesh['zh'=8,'zl'=2,'xh'=2,'xl'=2,'narrow'=8] {'zh','zl','xh','xl'}, dimensions={0} | all-to-all | bytes 1048576 | tf_op jit(solution)/shard_map/all_to_all | solution.py:382
  55.2 0.0 copy-done
  55.2 0.0 copy-done.2
  55.2 0.0 copy-done.3
  55.3 0.0 copy-done.5
  55.3 0.4 shard_map.137
  55.7 17.8 %all_to_all.46 = s16[16,72,128]{2,1,0:T(8,128)(2,1)S(1)} all-to-all(s16[16,72,128]{2,1,0:T(8,128)(2,1)S(1)} %get-tuple-element.21), channel_id=1, replica_groups=mesh['zh'=8,'zl'=2,'xh'=2,'xl'=2,'narrow'=8] {'zh','zl'}, dimensions={0} | all-to-all | bytes 589824 | tf_op jit(solution)/shard_map/all_to_all | solution.py:426
  73.5 0.2 broadcast_in_dim.23
  73.7 14.5 %all_to_all.47.packed_ref = s16[4,16,72,128]{3,2,1,0:T(8,128)(2,1)S(1)} all-to-all(s16[4,16,72,128]{3,2,1,0:T(8,128)(2,1)S(1)} %broadcast_in_dim.23), channel_id=1, replica_groups=mesh['zh'=8,'zl'=2,'xh'=2,'xl'=2,'narrow'=8] {'xh','xl'}, dimensions={0} | all-to-all | bytes 2359296 | tf_op jit(solution)/shard_map/all_to_all | solution.py:431
  88.2 2.6 %shard_map.138 = f32[8,72,128]{2,1,0:T(8,128)S(1)} custom-call(bf16[1024,4096]{1,0:T(8,128)(2,1)S(1)} %get-tuple-element.14.panel_ref, f32[8,512]{1,0:T(8,128)S(1)} %get-tuple-element.16.sums_ref, s16[4,16,72,128]{3,2,1,0:T(8,128)(2,1)S(1)} %all_to_all.47.packed_ref), custom_call_target="tpu_custom_call" | custom-call | flops 2147483648 | bytes 10485760 | tf_op jit(solution)/shard_map/pallas_call | solution.py:399
  90.9 19.9 %all_to_all.48.received_ref = f32[8,72,128]{2,1,0:T(8,128)S(1)} all-to-all(f32[8,72,128]{2,1,0:T(8,128)S(1)} %shard_map.138), channel_id=1, replica_groups=mesh['zh'=8,'zl'=2,'xh'=2,'xl'=2,'narrow'=8] {'narrow'}, dimensions={0} | all-to-all | bytes 589824 | tf_op jit(solution)/shard_map/all_to_all | solution.py:439
  110.8 0.2 shard_map.139
  111.0 23.7 %all_to_all.49 = s16[16,72,128]{2,1,0:T(8,128)(2,1)S(1)} all-to-all(s16[16,72,128]{2,1,0:T(8,128)(2,1)S(1)} %shard_map.139), channel_id=1, replica_groups=mesh['zh'=8,'zl'=2,'xh'=2,'xl'=2,'narrow'=8] {'zh','zl'}, dimensions={0} | all-to-all | bytes 589824 | tf_op jit(solution)/shard_map/all_to_all | solution.py:426
  134.8 12.5 %all-gather.2 = s16[64,72,128]{2,1,0:T(8,128)(2,1)S(1)} all-gather(s16[16,72,128]{2,1,0:T(8,128)(2,1)S(1)} %all_to_all.49), channel_id=2, replica_groups=mesh['zh'=8,'zl'=2,'xh'=2,'xl'=2,'narrow'=8] {'xh','xl'}, dimensions={0}, use_global_device_ids=true | all-gather | bytes 1474560 | tf_op jit(solution)/shard_map/all_gather | solution.py:428
  147.3 3.6 %shard_map.140 = f32[8,72,128]{2,1,0:T(8,128)S(1)} custom-call(bf16[1024,4096]{1,0:T(8,128)(2,1)S(1)} %get-tuple-element.14.panel_ref, f32[128,128,128]{2,1,0:T(8,128)S(1)} %get-tuple-element.15.sums_ref, s16[4,16,72,128]{3,2,1,0:T(8,128)(2,1)S(1)} %bitcast.14), custom_call_target="tpu_custom_call" | custom-call | flops 2147483648 | bytes 10485760 | tf_op jit(solution)/shard_map/pallas_call | solution.py:399
  150.9 18.1 %all_to_all.50.received_ref = f32[8,72,128]{2,1,0:T(8,128)S(1)} all-to-all(f32[8,72,128]{2,1,0:T(8,128)S(1)} %shard_map.140), channel_id=1, replica_groups=mesh['zh'=8,'zl'=2,'xh'=2,'xl'=2,'narrow'=8] {'narrow'}, dimensions={0} | all-to-all | bytes 589824 | tf_op jit(solution)/shard_map/all_to_all | solution.py:439
  169.0 0.2 shard_map.141
  169.2 27.9 %all_to_all.51 = s16[16,72,128]{2,1,0:T(8,128)(2,1)S(1)} all-to-all(s16[16,72,128]{2,1,0:T(8,128)(2,1)S(1)} %shard_map.141), channel_id=1, replica_groups=mesh['zh'=8,'zl'=2,'xh'=2,'xl'=2,'narrow'=8] {'zh','xh'}, dimensions={0} | all-to-all | bytes 589824 | tf_op jit(solution)/shard_map/all_to_all | solution.py:426
  197.1 0.2 broadcast_in_dim.24
  197.3 16.9 %all_to_all.52.packed_ref = s16[4,16,72,128]{3,2,1,0:T(8,128)(2,1)S(1)} all-to-all(s16[4,16,72,128]{3,2,1,0:T(8,128)(2,1)S(1)} %broadcast_in_dim.24), channel_id=1, replica_groups=mesh['zh'=8,'zl'=2,'xh'=2,'xl'=2,'narrow'=8] {'zl','xl'}, dimensions={0} | all-to-all | bytes 2359296 | tf_op jit(solution)/shard_map/all_to_all | solution.py:431
  214.2 0.0 copy-start.1
  214.2 0.0 copy-start.4
  214.2 3.6 %shard_map.142 = f32[8,72,128]{2,1,0:T(8,128)S(1)} custom-call(bf16[1024,4096]{1,0:T(8,128)(2,1)S(1)} %get-tuple-element.14.panel_ref, f32[128,128,128]{2,1,0:T(8,128)S(1)} %get-tuple-element.15.sums_ref, s16[4,16,72,128]{3,2,1,0:T(8,128)(2,1)S(1)} %all_to_all.52.packed_ref), custom_call_target="tpu_custom_call" | custom-call | flops 2147483648 | bytes 10485760 | tf_op jit(solution)/shard_map/pallas_call | solution.py:399
  217.8 13.4 %all_to_all.53.received_ref = f32[8,72,128]{2,1,0:T(8,128)S(1)} all-to-all(f32[8,72,128]{2,1,0:T(8,128)S(1)} %shard_map.142), channel_id=1, replica_groups=mesh['zh'=8,'zl'=2,'xh'=2,'xl'=2,'narrow'=8] {'narrow'}, dimensions={0} | all-to-all | bytes 589824 | tf_op jit(solution)/shard_map/all_to_all | solution.py:439
  231.1 0.0 copy-done.1
  231.1 0.0 copy-done.4
  231.1 0.8 shard_map.143
Async XLA Ops:
  0.7 54.6 %copy-start = (bf16[64,128]{1,0:T(8,128)(2,1)S(1)}, bf16[64,128]{1,0:T(8,128)(2,1)}, u32[]{:S(2)}) copy-start(bf16[64,128]{1,0:T(8,128)(2,1)} %features_ref.1) | copy-start | bytes 49156
  0.7 54.6 %copy-start.2 = (bf16[128,128]{1,0:T(8,128)(2,1)S(1)}, bf16[128,128]{1,0:T(8,128)(2,1)}, u32[]{:S(2)}) copy-start(bf16[128,128]{1,0:T(8,128)(2,1)} %w_self_ref.1) | copy-start | bytes 98308
  0.7 54.6 %copy-start.3 = (bf16[128,128]{1,0:T(8,128)(2,1)S(1)}, bf16[128,128]{1,0:T(8,128)(2,1)}, u32[]{:S(2)}) copy-start(bf16[128,128]{1,0:T(8,128)(2,1)} %w_neigh_ref.1) | copy-start | bytes 98308
  0.7 54.6 %copy-start.5 = (f32[128]{0:T(128)S(1)}, f32[128]{0:T(128)}, u32[]{:S(2)}) copy-start(f32[128]{0:T(128)} %param.20) | copy-start | bytes 1540
  214.2 17.0 %copy-start.1 = (bf16[128,256]{1,0:T(8,128)(2,1)S(1)}, bf16[128,256]{1,0:T(8,128)(2,1)}, u32[]{:S(2)}) copy-start(bf16[128,256]{1,0:T(8,128)(2,1)} %w_ref.1) | copy-start | bytes 196612
  214.2 17.0 %copy-start.4 = (f32[256]{0:T(256)S(1)}, f32[256]{0:T(256)}, u32[]{:S(2)}) copy-start(f32[256]{0:T(256)} %param.22) | copy-start | bytes 3076

commit v7 on v5

--- a/solution.py
+++ b/solution.py
@@ -20,14 +20,18 @@
 i16 = jnp.int16
 
 
-def call(body, out_shape, n_in, scratch=(), in_specs=None, flops=0, nbytes=0, limit=24 << 20):
+def call(
+    body, out_shape, n_in, scratch=(), in_specs=None, flops=0, nbytes=0, limit=24 << 20, away=0
+):
     vmem = pl.BlockSpec(memory_space=pltpu.VMEM)
     outs = out_shape if isinstance(out_shape, (list, tuple)) else [out_shape]
     return pl.pallas_call(
         body,
         out_shape=out_shape,
         in_specs=in_specs or [vmem] * n_in,
-        out_specs=[vmem] * len(outs) if isinstance(out_shape, (list, tuple)) else vmem,
+        out_specs=[pl.BlockSpec(memory_space=pltpu.HBM)] * away + [vmem] * (len(outs) - away)
+        if isinstance(out_shape, (list, tuple))
+        else vmem,
         scratch_shapes=list(scratch),
         compiler_params=pltpu.CompilerParams(vmem_limit_bytes=limit),
         cost_estimate=pl.CostEstimate(flops=flops, bytes_accessed=nbytes, transcendentals=0),
@@ -73,64 +77,24 @@
         out_ref[k] = packed
 
 
-def head_kernel(
+def pick_kernel(
     count_hbm,
     send_hbm,
     features_hbm,
-    rows_hbm,
-    cols_hbm,
-    used_hbm,
-    tiles_hbm,
-    linked_hbm,
-    dangling_hbm,
     outgoing_ref,
-    panel_ref,
-    total,
-    sums_ref,
-    own_ref,
-    far_ref,
-    marks_ref,
     count_ref,
     send_ref,
     features_ref,
-    rows_ref,
-    cols_ref,
-    used_ref,
-    tiles_ref,
-    linked_ref,
-    dangling_ref,
     turned_ref,
     index_ref,
-    whole_ref,
     sems,
 ):
-    pairs = (
-        (count_hbm, count_ref),
-        (send_hbm, send_ref),
-        (features_hbm, features_ref),
-        (linked_hbm, linked_ref),
-        (dangling_hbm, dangling_ref),
-        (rows_hbm, rows_ref),
-        (cols_hbm, cols_ref),
-        (used_hbm, used_ref),
-        (tiles_hbm, tiles_ref),
-    )
+    pairs = ((count_hbm, count_ref), (send_hbm, send_ref), (features_hbm, features_ref))
     loads = [pltpu.make_async_copy(a, b, sems.at[k]) for k, (a, b) in enumerate(pairs)]
     for load in loads:
         load.start()
-
-    row_tiles = panel_ref.shape[0] // 256
-    col_tiles = panel_ref.shape[1] // 128
-    zero = jnp.zeros((128, 128), f32)
-
-    def clear(p, _):
-        total[p] = zero
-        return 0
-
-    lax.fori_loop(0, row_tiles * col_tiles, clear, 0)
-    for load in loads[:5]:
+    for load in loads:
         load.wait()
-
     features = features_ref[...]
     nodes = features.shape[0]
     capacity, lists = send_ref.shape
@@ -155,10 +119,61 @@
         chosen = (row == index).astype(f32).astype(bf16)
         outgoing_ref[pl.ds(k * 128, 128), :] = dot(chosen, features, ((0,), (0,))).astype(bf16)
 
+
+def panel_kernel(
+    rows_hbm,
+    cols_hbm,
+    used_hbm,
+    tiles_hbm,
+    linked_hbm,
+    dangling_hbm,
+    panel_hbm,
+    total_hbm,
+    sums_ref,
+    own_ref,
+    far_ref,
+    marks_ref,
+    rows_ref,
+    cols_ref,
+    used_ref,
+    tiles_ref,
+    linked_ref,
+    dangling_ref,
+    whole_ref,
+    panel_ref,
+    total,
+    sems,
+):
+    pairs = (
+        (linked_hbm, linked_ref),
+        (dangling_hbm, dangling_ref),
+        (rows_hbm, rows_ref),
+        (cols_hbm, cols_ref),
+        (used_hbm, used_ref),
+        (tiles_hbm, tiles_ref),
+    )
+    loads = [pltpu.make_async_copy(a, b, sems.at[k]) for k, (a, b) in enumerate(pairs)]
+    for load in loads:
+        load.start()
+
+    nodes = own_ref.shape[0]
+    row_tiles = panel_ref.shape[0] // 256
+    col_tiles = panel_ref.shape[1] // 128
+    zero = jnp.zeros((128, 128), f32)
+
+    def clear(p, _):
+        total[p] = zero
+        return 0
+
+    lax.fori_loop(0, row_tiles * col_tiles, clear, 0)
+    for load in loads[:2]:
+        load.wait()
+
     same = lax.broadcasted_iota(i32, (nodes, nodes), 0) == lax.broadcasted_iota(
         i32, (nodes, nodes), 1
     )
     eye = same.astype(f32).astype(bf16)
+    over = ((1,), (1,))
     linked = linked_ref[...]
     high = linked >> 6
     linked = 64.0 * dot(eye, high.astype(f32).astype(bf16), over) + dot(
@@ -183,7 +198,7 @@
     marks_ref[pl.ds(nodes, 8), :] = jnp.zeros((8, 128), f32)
     marks_ref[pl.ds(nodes, 8), pl.ds(0, nodes)] = jnp.broadcast_to(mark, (8, nodes))
 
-    for load in loads[5:]:
+    for load in loads[2:]:
         load.wait()
 
     def place(t, _):
@@ -192,6 +207,9 @@
         return 0
 
     lax.fori_loop(0, used_ref[0, 0], place, 0)
+
+    kept = pltpu.make_async_copy(total, total_hbm, sems.at[6])
+    kept.start()
 
     def store(g, _):
         at = pl.ds(pl.multiple_of(g * 16, 16), 16)
@@ -209,6 +227,10 @@
     lax.fori_loop(0, row_tiles * 8, store, 0)
     for r in range(row_tiles):
         sums_ref[:, pl.ds(r * 128, 128)] = lane_sums(whole_ref[pl.ds(r * 128, 128), :])
+    moved = pltpu.make_async_copy(panel_ref, panel_hbm, sems.at[7])
+    moved.start()
+    kept.wait()
+    moved.wait()
 
 
 def hidden_kernel(
@@ -233,9 +255,33 @@
     encode(hidden, jnp.ones((1, hidden.shape[1]), f32), dangling_ref[...], out_ref)
 
 
+def first_spread_kernel(
+    node_total, parts, panel_hbm, sums_ref, packed_ref, out_ref, panel_ref, z_parts, s_row, sems
+):
+    piece = panel_ref.shape[0] // 4
+    loads = [
+        pltpu.make_async_copy(
+            panel_hbm.at[pl.ds(k * piece, piece)], panel_ref.at[pl.ds(k * piece, piece)], sems.at[k]
+        )
+        for k in range(4)
+    ]
+    for load in loads:
+        load.start()
+    spread_body(node_total, parts, loads, None, panel_ref, sums_ref, packed_ref, out_ref, z_parts, s_row)
+
+
 def spread_kernel(
-    node_total, parts, first, panel_ref, sums_ref, packed_ref, out_ref, z_parts, s_row
-):
+    node_total, parts, panel_ref, total_hbm, packed_ref, out_ref, z_parts, s_row, total, sems
+):
+    load = pltpu.make_async_copy(total_hbm, total, sems.at[0])
+    load.start()
+    spread_body(node_total, parts, (), load, panel_ref, total, packed_ref, out_ref, z_parts, s_row)
+
+
+def spread_body(
+    node_total, parts, loads, sums_load, panel_ref, sums_ref, packed_ref, out_ref, z_parts, s_row
+):
+    first = sums_load is None
     zh, zl, nx = parts
     half = panel_ref.shape[0] // 2
     nodes = 64
@@ -259,8 +305,18 @@
         before = extra[1:2]
     d_all = d_all * (1.0 / node_total)
     ds_all = ds_all * (1.0 / node_total)
-    upper = dot(panel_ref[:half], z_parts[...])
-    lower = dot(panel_ref[half:], z_parts[...])
+    if first:
+        piece = half // 2
+        done = []
+        for k, load in enumerate(loads):
+            load.wait()
+            done.append(dot(panel_ref[pl.ds(k * piece, piece), :], z_parts[...]))
+        upper = jnp.concatenate(done[:2], axis=0)
+        lower = jnp.concatenate(done[2:], axis=0)
+    else:
+        upper = dot(panel_ref[:half], z_parts[...])
+        lower = dot(panel_ref[half:], z_parts[...])
+        sums_load.wait()
     z_sum = (upper[:, :128] + upper[:, 128:]) + (lower[:, :128] + lower[:, 128:]) + d_all
     if first:
         s_sum = sums_ref[...]
@@ -339,41 +395,54 @@
     degree = neighbors.shape[1]
 
     keep = functools.partial(pltpu.with_memory_space_constraint, memory_space=pltpu.HBM)
-    outgoing, panel, total, row_sums, own, far, marks = call(
-        head_kernel,
+    hbm = pl.BlockSpec(memory_space=pltpu.HBM)
+    vmem = pl.BlockSpec(memory_space=pltpu.VMEM)
+    panel_shape = (2 * row_total, col_total)
+    total_shape = (row_total * col_total // (128 * 128), 128, 128)
+    outgoing = call(
+        pick_kernel,
+        shape((slots, width), bf16),
+        3,
+        in_specs=[hbm] * 3,
+        scratch=[
+            pltpu.SMEM((1, wide), i32),
+            pltpu.VMEM((capacity, wide), i32),
+            pltpu.VMEM((nodes, width), bf16),
+            pltpu.VMEM((wide, capacity), i32),
+            pltpu.VMEM((wide * capacity // 128, 128), i32),
+            pltpu.SemaphoreType.DMA((3,)),
+        ],
+        limit=4 << 20,
+    )(keep(send_count[0]), keep(send_rows[0, 0].T), keep(features))
+    panel, total, row_sums, own, far, marks = call(
+        panel_kernel,
         [
-            shape((slots, width), bf16),
-            shape((2 * row_total, col_total), bf16),
-            shape((row_total * col_total // (128 * 128), 128, 128), f32),
+            pltpu.HBM(panel_shape, bf16),
+            pltpu.HBM(total_shape, f32),
             shape((8, row_total), f32),
             shape((nodes, nodes), bf16),
             shape((nodes, slots), bf16),
             shape((nodes + 8, 128), f32),
         ],
-        9,
-        in_specs=[pl.BlockSpec(memory_space=pltpu.HBM)] * 9,
+        6,
+        in_specs=[hbm] * 6,
+        away=2,
         scratch=[
-            pltpu.SMEM((1, wide), i32),
-            pltpu.VMEM((capacity, wide), i32),
-            pltpu.VMEM((nodes, width), bf16),
             pltpu.SMEM(tile_rows.shape[1:], i32),
             pltpu.SMEM(tile_rows.shape[1:], i32),
             pltpu.SMEM((1, 1), i32),
             pltpu.VMEM(tiles.shape[2:], bf16),
             pltpu.VMEM((degree, nodes), i32),
             pltpu.VMEM((1, nodes), i32),
-            pltpu.VMEM((wide, capacity), i32),
-            pltpu.VMEM((wide * capacity // 128, 128), i32),
             pltpu.VMEM((row_total, 128), f32),
-            pltpu.SemaphoreType.DMA((9,)),
+            pltpu.VMEM(panel_shape, bf16),
+            pltpu.VMEM(total_shape, f32),
+            pltpu.SemaphoreType.DMA((8,)),
         ],
         flops=1 << 24,
         nbytes=20 << 20,
-        limit=16 << 20,
+        limit=24 << 20,
     )(
-        keep(send_count[0]),
-        keep(send_rows[0, 0].T),
-        keep(features),
         keep(tile_rows[0]),
         keep(tile_cols[0]),
         tile_count,
@@ -397,17 +466,27 @@
         limit=8 << 20,
     )(features, received, own, far, w_self, w_neigh, bias_hidden[None, :], marks)
 
-    def spread(packed, repeat):
-        return call(
-            functools.partial(spread_kernel, node_total, (zh, zl, nx), repeat == 0),
-            shape((narrow, nodes + 8, width), f32),
-            3,
-            scratch=[pltpu.VMEM((col_total, 2 * width), bf16), pltpu.VMEM((8, col_total), f32)],
-            flops=2 * 2 * row_total * col_total * 256,
-            nbytes=10 << 20,
-            limit=12 << 20,
-        )(panel, row_sums if repeat == 0 else total, packed)
-
+    partial_shape = shape((narrow, nodes + 8, width), f32)
+    z_scratch = [pltpu.VMEM((col_total, 2 * width), bf16), pltpu.VMEM((8, col_total), f32)]
+    cost = dict(flops=2 * 2 * row_total * col_total * 256, nbytes=10 << 20)
+    first_spread = call(
+        functools.partial(first_spread_kernel, node_total, (zh, zl, nx)),
+        [partial_shape, shape(panel_shape, bf16)],
+        3,
+        in_specs=[hbm, vmem, vmem],
+        scratch=z_scratch + [pltpu.SemaphoreType.DMA((4,))],
+        limit=16 << 20,
+        **cost,
+    )
+    spread = call(
+        functools.partial(spread_kernel, node_total, (zh, zl, nx)),
+        partial_shape,
+        3,
+        in_specs=[vmem, hbm, vmem],
+        scratch=z_scratch + [pltpu.VMEM(total_shape, f32), pltpu.SemaphoreType.DMA((1,))],
+        limit=20 << 20,
+        **cost,
+    )
     for repeat in range(ITERS):
         got = lax.all_to_all(packed, "zh", split_axis=0, concat_axis=0, tiled=True)
         got = lax.all_to_all(
@@ -418,7 +497,10 @@
             tiled=True,
         )
         got = got.reshape((zl, nx) + got.shape[1:])
-        partial = spread(got, repeat)
+        if repeat == 0:
+            partial, near = first_spread(keep(panel), row_sums, got)
+        else:
+            partial = spread(near, keep(total), got)
         sums = lax.all_to_all(partial, "narrow", split_axis=0, concat_axis=0, tiled=True)
         if repeat < ITERS - 1:
             packed = call(step_kernel, packed_shape, 3, limit=4 << 20)(sums, hidden, marks)

time: 217 us -> 223 us (1.028)
  blocking collectives: 199 us -> 148 us
  waiting for transfers between devices: 0 us -> 21.3 us
  starting transfers between devices: 0 us -> 19.1 us
  Pallas kernels: 16.6 us -> 32 us
    all_to_all x1 -> x0, blocking collectives: 49.4 us -> none  [body(): lax.all_to_all(outgoing.reshape(wide, capacity, width), ('zh', 'zl', 'x')...]
    all_to_all x0 -> x1, waiting for transfers between devices: none -> 21.3 us  [body(): lax.all_to_all(outgoing.reshape(wide, capacity, width), ('zh', 'zl', 'x')...]
    all_to_all x0 -> x1, starting transfers between devices: none -> 19.1 us  [body(): lax.all_to_all(outgoing.reshape(wide, capacity, width), ('zh', 'zl', 'x')...]
    pallas_call x4 -> x5, Pallas kernels: 15 us -> 30.4 us  [the longest x2 13.8 us: body(): partial = spread(near, keep(total), got)]
  transfers between devices with their start and end apart: 0 -> 1, of which waited for: 0 -> 1; matrix products, arithmetic and copies ran while one was open for 0% -> 0% of each run, Pallas kernels for 0% -> 4%
where the time goes in v7:
time: 223 us; the launch traced here: 222 us
  blocking collectives  148 us (66%)
  Pallas kernels  32 us (14%)
  waiting for transfers between devices  21.3 us (10%)
  starting transfers between devices  19.1 us (9%)
    all_to_all x3, blocking collectives, body(): got = lax.all_to_all(packed, 'zh', split_axis=0, concat_axis=0, tiled=True)  55.1 us
    all_to_all x3, blocking collectives, body(): lax.all_to_all(jnp.broadcast_to(got[None], (zl * nx,) + got.shape), ('zl'...  47.4 us
    all_to_all x3, blocking collectives, body(): lax.all_to_all(partial, 'narrow', split_axis=0, concat_axis=0, tiled=True)  45.7 us
    all_to_all x1, waiting for transfers between devices, body(): lax.all_to_all(outgoing.reshape(wide, capacity, width), ('zh', 'zl', 'x')...  21.3 us
    all_to_all x1, starting transfers between devices, body(): lax.all_to_all(outgoing.reshape(wide, capacity, width), ('zh', 'zl', 'x')...  19.1 us
    pallas_call x2, Pallas kernels, body(): partial = spread(near, keep(total), got)  13.8 us
    pallas_call x1, Pallas kernels, body(): call(panel_kernel, [pltpu.HBM(panel_shape, bf16), pltpu.HBM(total_shape,...  7.96 us
    pallas_call x1, Pallas kernels, body(): partial, near = first_spread(keep(panel), row_sums, got)  6.55 us
  transfers between devices with their start and end apart: 1, of which 1 were waited for; matrix products, arithmetic and copies ran while one was open for 0% of the time, Pallas kernels for 4%

profile of v7, /device:TPU:1, one launch (start us, length us, event | category | flops | bytes accessed | tf_op | source)
XLA Modules:
  0.0 222.0 jit_solution(14344596602734755247)
XLA Ops:
  0.0 2.2 shard_map.137
  2.2 19.1 %all-to-all-start = ((bf16[64,32,128]{2,1,0:T(8,128)(2,1)}), bf16[64,32,128]{2,1,0:T(8,128)(2,1)S(1)}, u32[]{:S(2)}, u32[]{:S(2)}) async-start(bf16[64,32,128]{2,1,0:T(8,128)(2,1)} %bitcast.8), calls=%async_computation | async-start | bytes 1048576 | tf_op jit(solution)/shard_map/all_to_all | solution.py:453
  21.3 0.0 copy-start
  21.3 0.0 copy-start.2
  21.3 0.0 copy-start.3
  21.3 0.0 copy-start.5
  22.0 8.0 %shard_map.136 = (bf16[1024,4096]{1,0:T(8,128)(2,1)}, f32[128,128,128]{2,1,0:T(8,128)}, f32[8,512]{1,0:T(8,128)S(1)}, bf16[64,64]{1,0:T(8,128)(2,1)S(1)}, bf16[6...) custom-call(s32[1,64]{1,0:T(1,128)} %bitcast.26, s32[1,64]{1,0:T(1,128)} %bitcast.27, s32[1,1]{1,0:T(1,128)S(6)} %copy.15.used_hbm, ...), custom_call_target="tpu_custom_call" | custom-call | flops 16777216 | bytes 20971520 | tf_op jit(solution)/shard_map/pallas_call | solution.py:417
  30.0 21.3 %all-to-all-done = bf16[64,32,128]{2,1,0:T(8,128)(2,1)S(1)} async-done(((bf16[64,32,128]{2,1,0:T(8,128)(2,1)}), bf16[64,32,128]{2,1,0:T(8,128)(2,1)S(1)}, u32[]{:S(2)}, u32[]{:S(2)}) %all-to-all-start) | async-done | bytes 524320 | tf_op jit(solution)/shard_map/all_to_all | solution.py:453
  51.3 0.0 copy-done
  51.3 0.0 copy-done.2
  51.3 0.0 copy-done.3
  51.3 0.0 copy-done.5
  51.3 0.4 shard_map.138
  51.8 18.4 %all_to_all.50 = s16[8,72,128]{2,1,0:T(8,128)(2,1)S(1)} all-to-all(s16[8,72,128]{2,1,0:T(8,128)(2,1)S(1)} %get-tuple-element.20), channel_id=1, replica_groups=mesh['zh'=8,'zl'=2,'x'=4,'narrow'=8] {'zh'}, dimensions={0} | all-to-all | bytes 294912 | tf_op jit(solution)/shard_map/all_to_all | solution.py:491
  70.2 0.2 broadcast_in_dim.14
  70.3 15.4 %all_to_all.51 = s16[8,8,72,128]{3,2,1,0:T(8,128)(2,1)S(1)} all-to-all(s16[8,8,72,128]{3,2,1,0:T(8,128)(2,1)S(1)} %broadcast_in_dim.14), channel_id=1, replica_groups=mesh['zh'=8,'zl'=2,'x'=4,'narrow'=8] {'zl','x'}, dimensions={0} | all-to-all | bytes 2359296 | tf_op jit(solution)/shard_map/all_to_all | solution.py:492
  85.7 6.5 %shard_map.139 = (f32[8,72,128]{2,1,0:T(8,128)S(1)}, bf16[1024,4096]{1,0:T(8,128)(2,1)S(1)}) custom-call(bf16[1024,4096]{1,0:T(8,128)(2,1)} %get-tuple-element.15.panel_hbm, f32[8,512]{1,0:T(8,128)S(1)} %get-tuple-element.16.sums_ref, s16[2,4,8,72,128]{4,3,2,1,0:T(8,128)(2,1)S(1)} %bitcast.16), custom_call_target="tpu_custom_call" | custom-call | flops 2147483648 | bytes 10485760 | tf_op jit(solution)/shard_map/pallas_call | solution.py:501
  92.3 17.4 %all_to_all.52.received_ref = f32[8,72,128]{2,1,0:T(8,128)S(1)} all-to-all(f32[8,72,128]{2,1,0:T(8,128)S(1)} %get-tuple-element.23), channel_id=1, replica_groups=mesh['zh'=8,'zl'=2,'x'=4,'narrow'=8] {'narrow'}, dimensions={0} | all-to-all | bytes 589824 | tf_op jit(solution)/shard_map/all_to_all | solution.py:504
  109.7 0.2 shard_map.140
  109.9 17.7 %all_to_all.53 = s16[8,72,128]{2,1,0:T(8,128)(2,1)S(1)} all-to-all(s16[8,72,128]{2,1,0:T(8,128)(2,1)S(1)} %shard_map.140), channel_id=1, replica_groups=mesh['zh'=8,'zl'=2,'x'=4,'narrow'=8] {'zh'}, dimensions={0} | all-to-all | bytes 294912 | tf_op jit(solution)/shard_map/all_to_all | solution.py:491
  127.6 0.2 broadcast_in_dim.30
  127.7 16.0 %all_to_all.54 = s16[8,8,72,128]{3,2,1,0:T(8,128)(2,1)S(1)} all-to-all(s16[8,8,72,128]{3,2,1,0:T(8,128)(2,1)S(1)} %broadcast_in_dim.30), channel_id=1, replica_groups=mesh['zh'=8,'zl'=2,'x'=4,'narrow'=8] {'zl','x'}, dimensions={0} | all-to-all | bytes 2359296 | tf_op jit(solution)/shard_map/all_to_all | solution.py:492
  143.7 6.9 %shard_map.141 = f32[8,72,128]{2,1,0:T(8,128)S(1)} custom-call(bf16[1024,4096]{1,0:T(8,128)(2,1)S(1)} %get-tuple-element.21.panel_ref, f32[128,128,128]{2,1,0:T(8,128)} %get-tuple-element.22.total_hbm, s16[2,4,8,72,128]{4,3,2,1,0:T(8,128)(2,1)S(1)} %bitcast.17), custom_call_target="tpu_custom_call" | custom-call | flops 2147483648 | bytes 10485760 | tf_op jit(solution)/shard_map/pallas_call | solution.py:503
  150.6 14.2 %all_to_all.55.received_ref = f32[8,72,128]{2,1,0:T(8,128)S(1)} all-to-all(f32[8,72,128]{2,1,0:T(8,128)S(1)} %shard_map.141), channel_id=1, replica_groups=mesh['zh'=8,'zl'=2,'x'=4,'narrow'=8] {'narrow'}, dimensions={0} | all-to-all | bytes 589824 | tf_op jit(solution)/shard_map/all_to_all | solution.py:504
  164.8 0.2 shard_map.142
  165.0 19.0 %all_to_all.56 = s16[8,72,128]{2,1,0:T(8,128)(2,1)S(1)} all-to-all(s16[8,72,128]{2,1,0:T(8,128)(2,1)S(1)} %shard_map.142), channel_id=1, replica_groups=mesh['zh'=8,'zl'=2,'x'=4,'narrow'=8] {'zh'}, dimensions={0} | all-to-all | bytes 294912 | tf_op jit(solution)/shard_map/all_to_all | solution.py:491
  184.0 0.2 broadcast_in_dim.31
  184.2 16.0 %all_to_all.57 = s16[8,8,72,128]{3,2,1,0:T(8,128)(2,1)S(1)} all-to-all(s16[8,8,72,128]{3,2,1,0:T(8,128)(2,1)S(1)} %broadcast_in_dim.31), channel_id=1, replica_groups=mesh['zh'=8,'zl'=2,'x'=4,'narrow'=8] {'zl','x'}, dimensions={0} | all-to-all | bytes 2359296 | tf_op jit(solution)/shard_map/all_to_all | solution.py:492
  200.2 0.0 copy-start.1
  200.2 0.0 copy-start.4
  200.2 6.9 %shard_map.143 = f32[8,72,128]{2,1,0:T(8,128)S(1)} custom-call(bf16[1024,4096]{1,0:T(8,128)(2,1)S(1)} %get-tuple-element.21.panel_ref, f32[128,128,128]{2,1,0:T(8,128)} %get-tuple-element.22.total_hbm, s16[2,4,8,72,128]{4,3,2,1,0:T(8,128)(2,1)S(1)} %bitcast.18), custom_call_target="tpu_custom_call" | custom-call | flops 2147483648 | bytes 10485760 | tf_op jit(solution)/shard_map/pallas_call | solution.py:503
  207.1 14.1 %all_to_all.58.received_ref = f32[8,72,128]{2,1,0:T(8,128)S(1)} all-to-all(f32[8,72,128]{2,1,0:T(8,128)S(1)} %shard_map.143), channel_id=1, replica_groups=mesh['zh'=8,'zl'=2,'x'=4,'narrow'=8] {'narrow'}, dimensions={0} | all-to-all | bytes 589824 | tf_op jit(solution)/shard_map/all_to_all | solution.py:504
  221.2 0.0 copy-done.1
  221.2 0.0 copy-done.4
  221.2 0.8 shard_map.144
Async XLA Ops:
  2.2 49.2 %all-to-all-start = ((bf16[64,32,128]{2,1,0:T(8,128)(2,1)}), bf16[64,32,128]{2,1,0:T(8,128)(2,1)S(1)}, u32[]{:S(2)}, u32[]{:S(2)}) async-start(bf16[64,32,128]{2,1,0:T(8,128)(2,1)} %bitcast.8), calls=%async_computation | async-start | bytes 1048576 | tf_op jit(solution)/shard_map/all_to_all | solution.py:453
  21.3 30.0 %copy-start = (bf16[64,128]{1,0:T(8,128)(2,1)S(1)}, bf16[64,128]{1,0:T(8,128)(2,1)}, u32[]{:S(2)}) copy-start(bf16[64,128]{1,0:T(8,128)(2,1)} %features_ref.1) | copy-start | bytes 49156
  21.3 30.0 %copy-start.2 = (bf16[128,128]{1,0:T(8,128)(2,1)S(1)}, bf16[128,128]{1,0:T(8,128)(2,1)}, u32[]{:S(2)}) copy-start(bf16[128,128]{1,0:T(8,128)(2,1)} %w_self_ref.1) | copy-start | bytes 98308
  21.3 30.0 %copy-start.3 = (bf16[128,128]{1,0:T(8,128)(2,1)S(1)}, bf16[128,128]{1,0:T(8,128)(2,1)}, u32[]{:S(2)}) copy-start(bf16[128,128]{1,0:T(8,128)(2,1)} %w_neigh_ref.1) | copy-start | bytes 98308
  21.3 30.0 %copy-start.5 = (f32[128]{0:T(128)S(1)}, f32[128]{0:T(128)}, u32[]{:S(2)}) copy-start(f32[128]{0:T(128)} %param.20) | copy-start | bytes 1540
  200.2 21.0 %copy-start.1 = (bf16[128,256]{1,0:T(8,128)(2,1)S(1)}, bf16[128,256]{1,0:T(8,128)(2,1)}, u32[]{:S(2)}) copy-start(bf16[128,256]{1,0:T(8,128)(2,1)} %w_ref.1) | copy-start | bytes 196612
  200.2 21.0 %copy-start.4 = (f32[256]{0:T(256)S(1)}, f32[256]{0:T(256)}, u32[]{:S(2)}) copy-start(f32[256]{0:T(256)} %param.22) | copy-start | bytes 3076

commit v8 on v5

--- a/solution.py
+++ b/solution.py
@@ -245,7 +245,7 @@
     before = None
     for a in range(zh * zl * nx):
         h, m, x = a // (zl * nx), (a // nx) % zl, a % nx
-        codes = packed_ref[m, x, h].astype(i32).astype(f32)
+        codes = packed_ref[x, m, h].astype(i32).astype(f32)
         tail = codes[nodes:]
         step = jnp.exp2(tail * (1.0 / 256.0)) * (1.0 / TOP)
         hi, lo = split(codes[:nodes] * step[0:1])
@@ -412,12 +412,12 @@
         got = lax.all_to_all(packed, "zh", split_axis=0, concat_axis=0, tiled=True)
         got = lax.all_to_all(
             jnp.broadcast_to(got[None], (zl * nx,) + got.shape),
-            ("zl", "x"),
+            ("x", "zl"),
             split_axis=0,
             concat_axis=0,
             tiled=True,
         )
-        got = got.reshape((zl, nx) + got.shape[1:])
+        got = got.reshape((nx, zl) + got.shape[1:])
         partial = spread(got, repeat)
         sums = lax.all_to_all(partial, "narrow", split_axis=0, concat_axis=0, tiled=True)
         if repeat < ITERS - 1:

time: 217 us -> 216 us (level)
  no operation moved by 1% of the time
where the time goes in v8:
time: 216 us; the launch traced here: 215 us
  blocking collectives  197 us (91%)
  Pallas kernels  17.1 us (8%)
    all_to_all x3, blocking collectives, body(): got = lax.all_to_all(packed, 'zh', split_axis=0, concat_axis=0, tiled=True)  54.5 us
    all_to_all x1, blocking collectives, body(): lax.all_to_all(outgoing.reshape(wide, capacity, width), ('zh', 'zl', 'x')...  47.7 us
    all_to_all x3, blocking collectives, body(): lax.all_to_all(jnp.broadcast_to(got[None], (zl * nx,) + got.shape), ('x',...  47.5 us
    all_to_all x3, blocking collectives, body(): lax.all_to_all(partial, 'narrow', split_axis=0, concat_axis=0, tiled=True)  47.3 us
    pallas_call x3, Pallas kernels, spread(): call(functools.partial(spread_kernel, node_total, (zh, zl, nx), repeat ==...  9.84 us
    pallas_call x1, Pallas kernels, body(): call(head_kernel, [shape((slots, width), bf16), shape((2 * row_total, col...  5.61 us

profile of v8, /device:TPU:1, one launch (start us, length us, event | category | flops | bytes accessed | tf_op | source)
XLA Modules:
  0.0 215.3 jit_solution(8655865715422419738)
XLA Ops:
  0.7 0.0 copy-start
  0.7 0.0 copy-start.2
  0.7 0.0 copy-start.3
  0.7 0.0 copy-start.5
  0.7 5.6 %shard_map.136 = (bf16[2048,128]{1,0:T(8,128)(2,1)S(1)}, bf16[1024,4096]{1,0:T(8,128)(2,1)S(1)}, f32[128,128,128]{2,1,0:T(8,128)S(1)}, f32[8,512]{1,0:T(8,128)S(...) custom-call(s32[1,64]{1,0:T(1,128)} %bitcast.26, s32[32,64]{1,0:T(8,128)} %bitcast.24, ...), custom_call_target="tpu_custom_call" | custom-call | flops 16777216 | bytes 20971520 | tf_op jit(solution)/shard_map/pallas_call | solution.py:342
  6.3 47.7 %all_to_all.50 = bf16[64,32,128]{2,1,0:T(8,128)(2,1)S(1)} all-to-all(bf16[64,32,128]{2,1,0:T(8,128)(2,1)S(1)} %bitcast.20), channel_id=1, replica_groups=mesh['zh'=8,'zl'=2,'x'=4,'narrow'=8] {'zh','zl','x'}, dimensions={0} | all-to-all | bytes 1048576 | tf_op jit(solution)/shard_map/all_to_all | solution.py:384
  54.0 0.0 copy-done
  54.0 0.0 copy-done.2
  54.0 0.0 copy-done.3
  54.0 0.0 copy-done.5
  54.0 0.4 shard_map.137
  54.5 18.8 %all_to_all.51 = s16[8,72,128]{2,1,0:T(8,128)(2,1)S(1)} all-to-all(s16[8,72,128]{2,1,0:T(8,128)(2,1)S(1)} %get-tuple-element.21), channel_id=1, replica_groups=mesh['zh'=8,'zl'=2,'x'=4,'narrow'=8] {'zh'}, dimensions={0} | all-to-all | bytes 294912 | tf_op jit(solution)/shard_map/all_to_all | solution.py:412
  73.3 0.2 broadcast_in_dim.14
  73.4 15.8 %all_to_all.52 = s16[8,8,72,128]{3,2,1,0:T(8,128)(2,1)S(1)} all-to-all(s16[8,8,72,128]{3,2,1,0:T(8,128)(2,1)S(1)} %broadcast_in_dim.14), channel_id=1, replica_groups=mesh['zh'=8,'zl'=2,'x'=4,'narrow'=8] {'x','zl'}, dimensions={0} | all-to-all | bytes 2359296 | tf_op jit(solution)/shard_map/all_to_all | solution.py:413
  89.2 2.6 %shard_map.138 = f32[8,72,128]{2,1,0:T(8,128)S(1)} custom-call(bf16[1024,4096]{1,0:T(8,128)(2,1)S(1)} %get-tuple-element.14.panel_ref, f32[8,512]{1,0:T(8,128)S(1)} %get-tuple-element.16.sums_ref, s16[4,2,8,72,128]{4,3,2,1,0:T(8,128)(2,1)S(1)} %bitcast.17), custom_call_target="tpu_custom_call" | custom-call | flops 2147483648 | bytes 10485760 | tf_op jit(solution)/shard_map/pallas_call | solution.py:401
  91.9 18.4 %all_to_all.53.received_ref = f32[8,72,128]{2,1,0:T(8,128)S(1)} all-to-all(f32[8,72,128]{2,1,0:T(8,128)S(1)} %shard_map.138), channel_id=1, replica_groups=mesh['zh'=8,'zl'=2,'x'=4,'narrow'=8] {'narrow'}, dimensions={0} | all-to-all | bytes 589824 | tf_op jit(solution)/shard_map/all_to_all | solution.py:422
  110.3 0.2 shard_map.139
  110.5 17.4 %all_to_all.54 = s16[8,72,128]{2,1,0:T(8,128)(2,1)S(1)} all-to-all(s16[8,72,128]{2,1,0:T(8,128)(2,1)S(1)} %shard_map.139), channel_id=1, replica_groups=mesh['zh'=8,'zl'=2,'x'=4,'narrow'=8] {'zh'}, dimensions={0} | all-to-all | bytes 294912 | tf_op jit(solution)/shard_map/all_to_all | solution.py:412
  127.9 0.2 broadcast_in_dim.30
  128.1 15.8 %all_to_all.55 = s16[8,8,72,128]{3,2,1,0:T(8,128)(2,1)S(1)} all-to-all(s16[8,8,72,128]{3,2,1,0:T(8,128)(2,1)S(1)} %broadcast_in_dim.30), channel_id=1, replica_groups=mesh['zh'=8,'zl'=2,'x'=4,'narrow'=8] {'x','zl'}, dimensions={0} | all-to-all | bytes 2359296 | tf_op jit(solution)/shard_map/all_to_all | solution.py:413
  143.9 3.6 %shard_map.140 = f32[8,72,128]{2,1,0:T(8,128)S(1)} custom-call(bf16[1024,4096]{1,0:T(8,128)(2,1)S(1)} %get-tuple-element.14.panel_ref, f32[128,128,128]{2,1,0:T(8,128)S(1)} %get-tuple-element.15.sums_ref, s16[4,2,8,72,128]{4,3,2,1,0:T(8,128)(2,1)S(1)} %bitcast.18), custom_call_target="tpu_custom_call" | custom-call | flops 2147483648 | bytes 10485760 | tf_op jit(solution)/shard_map/pallas_call | solution.py:401
  147.5 14.5 %all_to_all.56.received_ref = f32[8,72,128]{2,1,0:T(8,128)S(1)} all-to-all(f32[8,72,128]{2,1,0:T(8,128)S(1)} %shard_map.140), channel_id=1, replica_groups=mesh['zh'=8,'zl'=2,'x'=4,'narrow'=8] {'narrow'}, dimensions={0} | all-to-all | bytes 589824 | tf_op jit(solution)/shard_map/all_to_all | solution.py:422
  162.0 0.2 shard_map.141
  162.2 18.3 %all_to_all.57 = s16[8,72,128]{2,1,0:T(8,128)(2,1)S(1)} all-to-all(s16[8,72,128]{2,1,0:T(8,128)(2,1)S(1)} %shard_map.141), channel_id=1, replica_groups=mesh['zh'=8,'zl'=2,'x'=4,'narrow'=8] {'zh'}, dimensions={0} | all-to-all | bytes 294912 | tf_op jit(solution)/shard_map/all_to_all | solution.py:412
  180.5 0.2 broadcast_in_dim.31
  180.6 15.8 %all_to_all.58 = s16[8,8,72,128]{3,2,1,0:T(8,128)(2,1)S(1)} all-to-all(s16[8,8,72,128]{3,2,1,0:T(8,128)(2,1)S(1)} %broadcast_in_dim.31), channel_id=1, replica_groups=mesh['zh'=8,'zl'=2,'x'=4,'narrow'=8] {'x','zl'}, dimensions={0} | all-to-all | bytes 2359296 | tf_op jit(solution)/shard_map/all_to_all | solution.py:413
  196.5 0.0 copy-start.1
  196.5 0.0 copy-start.4
  196.5 3.6 %shard_map.142 = f32[8,72,128]{2,1,0:T(8,128)S(1)} custom-call(bf16[1024,4096]{1,0:T(8,128)(2,1)S(1)} %get-tuple-element.14.panel_ref, f32[128,128,128]{2,1,0:T(8,128)S(1)} %get-tuple-element.15.sums_ref, s16[4,2,8,72,128]{4,3,2,1,0:T(8,128)(2,1)S(1)} %bitcast.16), custom_call_target="tpu_custom_call" | custom-call | flops 2147483648 | bytes 10485760 | tf_op jit(solution)/shard_map/pallas_call | solution.py:401
  200.1 14.5 %all_to_all.59.received_ref = f32[8,72,128]{2,1,0:T(8,128)S(1)} all-to-all(f32[8,72,128]{2,1,0:T(8,128)S(1)} %shard_map.142), channel_id=1, replica_groups=mesh['zh'=8,'zl'=2,'x'=4,'narrow'=8] {'narrow'}, dimensions={0} | all-to-all | bytes 589824 | tf_op jit(solution)/shard_map/all_to_all | solution.py:422
  214.5 0.0 copy-done.1
  214.5 0.0 copy-done.4
  214.5 0.8 shard_map.143
Async XLA Ops:
  0.7 53.4 %copy-start = (bf16[64,128]{1,0:T(8,128)(2,1)S(1)}, bf16[64,128]{1,0:T(8,128)(2,1)}, u32[]{:S(2)}) copy-start(bf16[64,128]{1,0:T(8,128)(2,1)} %features_ref.1) | copy-start | bytes 49156
  0.7 53.3 %copy-start.2 = (bf16[128,128]{1,0:T(8,128)(2,1)S(1)}, bf16[128,128]{1,0:T(8,128)(2,1)}, u32[]{:S(2)}) copy-start(bf16[128,128]{1,0:T(8,128)(2,1)} %w_self_ref.1) | copy-start | bytes 98308
  0.7 53.3 %copy-start.3 = (bf16[128,128]{1,0:T(8,128)(2,1)S(1)}, bf16[128,128]{1,0:T(8,128)(2,1)}, u32[]{:S(2)}) copy-start(bf16[128,128]{1,0:T(8,128)(2,1)} %w_neigh_ref.1) | copy-start | bytes 98308
  0.7 53.3 %copy-start.5 = (f32[128]{0:T(128)S(1)}, f32[128]{0:T(128)}, u32[]{:S(2)}) copy-start(f32[128]{0:T(128)} %param.20) | copy-start | bytes 1540
  196.5 18.1 %copy-start.1 = (bf16[128,256]{1,0:T(8,128)(2,1)S(1)}, bf16[128,256]{1,0:T(8,128)(2,1)}, u32[]{:S(2)}) copy-start(bf16[128,256]{1,0:T(8,128)(2,1)} %w_ref.1) | copy-start | bytes 196612
  196.5 18.1 %copy-start.4 = (f32[256]{0:T(256)S(1)}, f32[256]{0:T(256)}, u32[]{:S(2)}) copy-start(f32[256]{0:T(256)} %param.22) | copy-start | bytes 3076
